TPU v7x, 512 devices: a whole 4x4x16 slice. The times are simulated.
512 devices in a mesh: dp: 16 (over y, z_lo), ctx: 32 (over x, z_hi, core).
Axes of the slice: x: 4, y: 4, z: 16 (z_hi: 4, z_lo: 4; z = z_hi * 4 + z_lo), core: 2. Of those that a mesh axis runs over, the one named last changes fastest.
Arguments:
- queries: bfloat16 [16, 4096, 512], P('dp', 'ctx'), may hold values from -6 to 6
- keys: bfloat16 [16, 4096, 512], P('dp', 'ctx'), may hold values from -6 to 6
- values: bfloat16 [16, 4096, 512], P('dp', 'ctx'), may hold values from -6 to 6
- grad_out: bfloat16 [16, 4096, 512], P('dp', 'ctx'), may hold values from -6 to 6
- filter_taps: float32 [4096, 512], P('ctx'), may hold values from -0.125 to 0.125
Outputs:
- conv_out: bfloat16 [16, 4096, 512], P('dp', 'ctx')
- grad_queries: bfloat16 [16, 4096, 512], P('dp', 'ctx')
- grad_keys: bfloat16 [16, 4096, 512], P('dp', 'ctx')
- grad_values: bfloat16 [16, 4096, 512], P('dp', 'ctx')
- grad_filter: float32 [4096, 512], P('ctx')
All inputs are finite; a program needn't handle non-finite values.
Results may differ from a plain program's by a relative error of at most 0.0023.
Values sent between devices are 32-bit elements; how exact they have to be, the bound alone decides.
No kernel may reach another device: no remote copies, remote signals or barrier semaphores. Data moves between devices by JAX's collectives and lax.ppermute only.
A program may use at most 64 MiB of HBM per device.

v0:
```python
import math

import jax
import jax.numpy as jnp
from jax import lax
from jax.sharding import PartitionSpec as P


def angle_table(numer, denom):
    angle = 2.0 * math.pi / denom * (numer % denom).astype(jnp.float32)
    return (jnp.cos(angle), jnp.sin(angle))


def exact_dot(left, right):
    return jnp.dot(left, right, precision=lax.Precision.HIGHEST)


def exact_mix(table, operand):
    return jnp.einsum("kb,abc->akc", table, operand, precision=lax.Precision.HIGHEST)


def owned_harmonics(blocks):
    rows = lax.iota(jnp.int32, 2 * blocks)
    half_row = rows // 2
    mirrored = jnp.where(half_row == 0, blocks, 2 * blocks - half_row)
    return jnp.where(rows % 2 == 0, half_row, mirrored)


def forward_spectrum(real_in):
    blocks = lax.axis_size("ctx")
    tokens, width = real_in.shape
    stride = tokens // blocks
    period = 2 * blocks * tokens
    total_width = real_in.shape[1]
    columns = lax.all_to_all(
        real_in.reshape(1, tokens, total_width), "ctx", split_axis=1, concat_axis=0, tiled=True
    )
    harmonic = owned_harmonics(blocks)
    source = lax.iota(jnp.int32, blocks)
    cos_mix, sin_mix = angle_table(harmonic[:, None] * source[None, :], 2 * blocks)
    flat_real = columns.reshape(blocks, stride * width)
    real_part = exact_dot(cos_mix, flat_real)
    imag_part = -exact_dot(sin_mix, flat_real)
    real_part = real_part.reshape(2 * blocks, stride, width)
    imag_part = imag_part.reshape(2 * blocks, stride, width)
    offsets = lax.axis_index("ctx") * stride + lax.iota(jnp.int32, stride)
    cos_turn, sin_turn = angle_table(harmonic[:, None] * offsets[None, :], period)
    cos_turn = cos_turn[:, :, None]
    sin_turn = sin_turn[:, :, None]
    rotated = jnp.stack(
        [real_part * cos_turn + imag_part * sin_turn, imag_part * cos_turn - real_part * sin_turn]
    )
    spectral = lax.all_to_all(rotated, "ctx", split_axis=1, concat_axis=2, tiled=True)
    position = lax.iota(jnp.int32, tokens)
    cos_full, sin_full = angle_table(position[:, None] * position[None, :], tokens)
    out_real = exact_mix(cos_full, spectral[0]) + exact_mix(sin_full, spectral[1])
    out_imag = exact_mix(cos_full, spectral[1]) - exact_mix(sin_full, spectral[0])
    return (out_real, out_imag)


def transform_pairs(first, second):
    width = first.shape[1]
    all_real, all_imag = forward_spectrum(jnp.concatenate([first, second], 1))
    return (
        all_real[..., :width],
        all_imag[..., :width],
        all_real[..., width:],
        all_imag[..., width:],
    )


def inverse_tokens(spec_real, spec_imag):
    blocks = lax.axis_size("ctx")
    tokens = spec_real.shape[1]
    channels = spec_real.shape[2]
    stride = tokens // blocks
    period = 2 * blocks * tokens
    position = lax.iota(jnp.int32, tokens)
    cos_full, sin_full = angle_table(position[:, None] * position[None, :], tokens)
    back_real = exact_mix(cos_full, spec_real) - exact_mix(sin_full, spec_imag)
    back_imag = exact_mix(sin_full, spec_real) + exact_mix(cos_full, spec_imag)
    harmonic = owned_harmonics(blocks)
    local_freq = lax.dynamic_slice_in_dim(harmonic, 2 * lax.axis_index("ctx"), 2)
    cos_turn, sin_turn = angle_table(local_freq[:, None] * position[None, :], period)
    cos_turn = cos_turn[:, :, None]
    sin_turn = sin_turn[:, :, None]
    rotated = jnp.stack(
        [back_real * cos_turn - back_imag * sin_turn, back_real * sin_turn + back_imag * cos_turn]
    )
    gathered = lax.all_to_all(rotated, "ctx", split_axis=2, concat_axis=1, tiled=True)
    source = lax.iota(jnp.int32, blocks)
    cos_mix, sin_mix = angle_table(source[:, None] * harmonic[None, :], 2 * blocks)
    flat_real = gathered[0].reshape(2 * blocks, stride * channels)
    flat_imag = gathered[1].reshape(2 * blocks, stride * channels)
    finished = (exact_dot(cos_mix, flat_real) - exact_dot(sin_mix, flat_imag)) * (1.0 / period)
    finished = finished.reshape(blocks, stride, channels)
    returned = lax.all_to_all(finished, "ctx", split_axis=0, concat_axis=1, tiled=True)
    return returned.reshape(tokens, finished.shape[2])


def inverse_pairs(first_real, first_imag, second_real, second_imag):
    width = first_real.shape[2]
    timed = inverse_tokens(
        jnp.concatenate([first_real, second_real], 2), jnp.concatenate([first_imag, second_imag], 2)
    )
    return (timed[:, :width], timed[:, width:])


def local(queries, keys, values, grad_out, filter_taps):
    query_f = queries[0].astype(jnp.float32)
    key_f = keys[0].astype(jnp.float32)
    value_f = values[0].astype(jnp.float32)
    grad_f = grad_out[0].astype(jnp.float32)
    gated = key_f * value_f
    grad_s = grad_f * query_f
    channels = query_f.shape[1]
    half_width = channels // 2
    groups = lax.axis_size("dp")
    per_group = channels // groups
    half_group = per_group // 2
    gated_real, gated_imag, grad_real, grad_imag = transform_pairs(gated, grad_s)
    filter_part = lax.dynamic_slice_in_dim(
        filter_taps, lax.axis_index("dp") * per_group, per_group, 1
    )
    low_real, low_imag, high_real, high_imag = transform_pairs(
        filter_part[:, :half_group], filter_part[:, half_group:]
    )
    own_real = jnp.concatenate([low_real, high_real], 2)
    own_imag = jnp.concatenate([low_imag, high_imag], 2)
    taps_real, taps_imag = (
        lax.all_gather(own_real, "dp", axis=2, tiled=True),
        lax.all_gather(own_imag, "dp", axis=2, tiled=True),
    )
    conv_real = taps_real * gated_real - taps_imag * gated_imag
    conv_imag = taps_real * gated_imag + taps_imag * gated_real
    back_real = taps_real * grad_real + taps_imag * grad_imag
    back_imag = taps_real * grad_imag - taps_imag * grad_real
    lag_real = grad_real * gated_real + grad_imag * gated_imag
    lag_imag = grad_imag * gated_real - grad_real * gated_imag
    grad_scale = 1.0 / math.sqrt(groups * lax.axis_size("ctx") * query_f.shape[0])
    first_time, second_time = inverse_pairs(
        jnp.concatenate([conv_real, lag_real[..., :half_width]], 2),
        jnp.concatenate([conv_imag, lag_imag[..., :half_width]], 2),
        jnp.concatenate([back_real, lag_real[..., half_width:]], 2),
        jnp.concatenate([back_imag, lag_imag[..., half_width:]], 2),
    )
    conv_s = first_time[:, :channels]
    grad_z = second_time[:, :channels]
    lag_grad = jnp.concatenate([first_time[:, channels:], second_time[:, channels:]], 1)
    grad_filter = lax.psum(lag_grad, "dp") * grad_scale
    conv_out = (query_f * conv_s).astype(jnp.bfloat16)[None]
    grad_queries = (grad_f * conv_s).astype(jnp.bfloat16)[None]
    grad_keys = (grad_z * value_f).astype(jnp.bfloat16)[None]
    grad_values = (grad_z * key_f).astype(jnp.bfloat16)[None]
    return (conv_out, grad_queries, grad_keys, grad_values, grad_filter)


def solution(mesh):
    return jax.shard_map(
        local,
        mesh=mesh,
        in_specs=(
            P("dp", "ctx", None),
            P("dp", "ctx", None),
            P("dp", "ctx", None),
            P("dp", "ctx", None),
            P("ctx", None),
        ),
        out_specs=(
            P("dp", "ctx", None),
            P("dp", "ctx", None),
            P("dp", "ctx", None),
            P("dp", "ctx", None),
            P("ctx", None),
        ),
        check_vma=False,
    )
```

profile of v0, /device:TPU:2, one launch (start us, length us, event | category | flops | bytes accessed | tf_op | source)
XLA Modules:
  0.0 685.8 jit_solution(10451977138814739588)
XLA Ops:
  10.2 18.2 %all-to-all-start = ((f32[32,1,128]{2,1,0:T(1,128)}), f32[32,1,128]{2,1,0:T(1,128)S(1)}, u32[]{:S(2)}, u32[]{:S(2)}) async-start(f32[32,1,128]{2,1,0:T(1,128)} %reshape.270), calls=%async_computation | async-start | bytes 32768 | tf_op jit(solution)/shard_map/all_to_all | solution.py:35
  28.5 1.2 convert_multiply_fusion.1
  29.7 1.2 reshape.248
  30.9 10.9 %all-to-all-done = f32[32,1,128]{2,1,0:T(1,128)S(1)} async-done(((f32[32,1,128]{2,1,0:T(1,128)}), f32[32,1,128]{2,1,0:T(1,128)S(1)}, u32[]{:S(2)}, u32[]{:S(2)}) %all-to-all-start) | async-done | bytes 16416 | tf_op jit(solution)/shard_map/all_to_all | solution.py:35
  41.8 5.0 all-to-all-start.2
  51.0 22.9 %all-to-all-done.2 = f32[1,128,1024]{2,0,1:T(1,128)S(1)} async-done(((f32[1,128,1024]{2,0,1:T(1,128)}), f32[1,128,1024]{2,0,1:T(1,128)S(1)}, u32[]{:S(2)}, u32[]{:S(2)}) %all-to-all-start.2) | async-done | bytes 524320 | tf_op jit(solution)/shard_map/all_to_all | solution.py:35
  74.0 9.7 %all-to-all-start.1 = ((f32[32,1,512]{2,1,0:T(1,128)}), f32[32,1,512]{2,1,0:T(1,128)S(1)}, u32[]{:S(2)}, u32[]{:S(2)}) async-start(f32[32,1,512]{2,1,0:T(1,128)} %reshape.272), calls=%async_computation.1 | async-start | bytes 131072 | tf_op jit(solution)/shard_map/all_to_all | solution.py:53
  83.7 1.2 reduce.1
  85.2 1.1 convolution_negate_fusion
  86.3 1.3 fusion.6
  87.9 2.7 copy.46
  90.6 6.8 all-to-all-done.1
  97.4 7.8 %all-to-all-start.3 = ((f32[2,64,4,1024]{3,2,0,1:T(4,128)}), f32[2,64,4,1024]{3,2,0,1:T(4,128)S(1)}, u32[]{:S(2)}, u32[]{:S(2)}) async-start(f32[2,64,4,1024]{3,2,0,1:T(4,128)} %copy.46), calls=%async_computation.3 | async-start | bytes 4194304 | tf_op jit(solution)/shard_map/all_to_all | solution.py:53
  108.6 130.4 %all_gather.7 = f32[2,128,512]{1,2,0:T(8,128)} all-gather(f32[2,128,32]{1,2,0:T(8,128)S(1)} %fusion.3), channel_id=1, replica_groups=mesh['dp'=16,'ctx'=32] {'dp'}, dimensions={2}, use_global_device_ids=true | all-gather | bytes 557056 | tf_op jit(solution)/shard_map/all_gather | solution.py:132
  239.0 44.2 %all_gather.6 = f32[2,128,512]{1,2,0:T(8,128)} all-gather(f32[2,128,32]{1,2,0:T(8,128)S(1)} %fusion.4), channel_id=1, replica_groups=mesh['dp'=16,'ctx'=32] {'dp'}, dimensions={2}, use_global_device_ids=true | all-gather | bytes 557056 | tf_op jit(solution)/shard_map/all_gather | solution.py:131
  283.3 1.9 copy.75
  285.2 1.3 fusion.171
  287.5 1.2 fusion.33
  288.8 1.2 fusion.37
  290.0 1.2 fusion.1
  291.3 1.3 fusion.2
  293.0 1.7 fusion.9
  294.7 1.6 fusion.10
  296.4 1.7 convolution_add_fusion
  298.1 2.2 subtract_bitcast_fusion
  300.5 3.6 copy.54
  304.1 153.5 %all_to_all.72 = f32[2,2,128,1536]{3,1,0,2:T(2,128)S(1)} all-to-all(f32[2,2,128,1536]{3,1,0,2:T(2,128)} %copy.54), channel_id=1, replica_groups=mesh['dp'=16,'ctx'=32] {'ctx'}, dimensions={2} | all-to-all | bytes 6291456 | tf_op jit(solution)/shard_map/all_to_all | solution.py:90
  457.5 1.1 copy.55
  458.6 1.1 fusion.170
  463.9 50.3 %all_to_all.73 = f32[32,4,1536]{2,1,0:T(4,128)S(1)} all-to-all(f32[32,4,1536]{2,1,0:T(4,128)S(1)} %reshape.251), channel_id=1, replica_groups=mesh['dp'=16,'ctx'=32] {'ctx'}, dimensions={0} | all-to-all | bytes 1572864 | tf_op jit(solution)/shard_map/all_to_all | solution.py:97
  516.2 161.1 %all-reduce.2.cloned.1.call-done = f32[128,512]{1,0:T(8,128)} async-done(((f32[128,512]{1,0:T(8,128)}), f32[128,512]{1,0:T(8,128)}) %all-reduce.2.cloned.1.call-update) | async-done | bytes 262160 | tf_op jit(solution)/shard_map/psum | solution.py:150
  677.3 1.7 broadcast_multiply_fusion
  (68 shorter events, 18.8 us)
Async XLA Ops:
  7.2 1.0 copy-start
  10.2 31.6 %all-to-all-start = ((f32[32,1,128]{2,1,0:T(1,128)}), f32[32,1,128]{2,1,0:T(1,128)S(1)}, u32[]{:S(2)}, u32[]{:S(2)}) async-start(f32[32,1,128]{2,1,0:T(1,128)} %reshape.270), calls=%async_computation | async-start | bytes 32768 | tf_op jit(solution)/shard_map/all_to_all | solution.py:35
  41.8 32.2 %all-to-all-start.2 = ((f32[1,128,1024]{2,0,1:T(1,128)}), f32[1,128,1024]{2,0,1:T(1,128)S(1)}, u32[]{:S(2)}, u32[]{:S(2)}) async-start(f32[1,128,1024]{2,0,1:T(1,128)} %reshape.248), calls=%async_computation.2 | async-start | bytes 1048576 | tf_op jit(solution)/shard_map/all_to_all | solution.py:35
  74.0 23.4 %all-to-all-start.1 = ((f32[32,1,512]{2,1,0:T(1,128)}), f32[32,1,512]{2,1,0:T(1,128)S(1)}, u32[]{:S(2)}, u32[]{:S(2)}) async-start(f32[32,1,512]{2,1,0:T(1,128)} %reshape.272), calls=%async_computation.1 | async-start | bytes 131072 | tf_op jit(solution)/shard_map/all_to_all | solution.py:53
  97.4 185.9 %all-to-all-start.3 = ((f32[2,64,4,1024]{3,2,0,1:T(4,128)}), f32[2,64,4,1024]{3,2,0,1:T(4,128)S(1)}, u32[]{:S(2)}, u32[]{:S(2)}) async-start(f32[2,64,4,1024]{3,2,0,1:T(4,128)} %copy.46), calls=%async_computation.3 | async-start | bytes 4194304 | tf_op jit(solution)/shard_map/all_to_all | solution.py:53
  105.2 572.1 %all-reduce.2.cloned.1.call-start = ((), (), s32[]{:S(2)}) async-start(), calls=%async_computation.6 | async-start | bytes 524288 | tf_op jit(solution)/shard_map/psum | solution.py:150
  291.2 1.3 copy-start.1
  291.3 1.3 copy-start.2
  514.2 1.1 copy-start.3
  514.2 1.1 copy-start.4
  514.2 1.1 copy-start.5
  514.3 1.1 copy-start.6
Sparse Core Ops, SparseCore 0:
  515.4 161.7 all-reduce.1
where the time goes:
time: 686 us
  blocking collectives  378 us (55%)
  waiting for transfers between devices  202 us (29%)
  starting transfers between devices  40.8 us (6%)
  local copies, waits for them, and re-layouts  22.2 us (3%)
  matrix products  19 us (3%)
  between operations  14.6 us (2%)
  other arithmetic  9.08 us (1%)
    psum x1, waiting for transfers between devices, local(): grad_filter = lax.psum(lag_grad, 'dp') * grad_scale  161 us
    all_to_all x1, blocking collectives, inverse_tokens(): lax.all_to_all(rotated, 'ctx', split_axis=2, concat_axis=1, tiled=True)  153 us
    all_gather x1, blocking collectives, local(): lax.all_gather(own_imag, 'dp', axis=2, tiled=True)  130 us
    all_to_all x1, blocking collectives, inverse_tokens(): lax.all_to_all(finished, 'ctx', split_axis=0, concat_axis=1, tiled=True)  50.3 us
    all_gather x1, blocking collectives, local(): lax.all_gather(own_real, 'dp', axis=2, tiled=True)  44.2 us
    all_to_all x2, waiting for transfers between devices, forward_spectrum(): lax.all_to_all(real_in.reshape(1, tokens, total_width), 'ctx', split_axis...  33.9 us
    all_to_all x2, starting transfers between devices, forward_spectrum(): lax.all_to_all(real_in.reshape(1, tokens, total_width), 'ctx', split_axis...  23.2 us
    all_to_all x2, starting transfers between devices, forward_spectrum(): lax.all_to_all(rotated, 'ctx', split_axis=1, concat_axis=2, tiled=True)  17.5 us
  transfers between devices with their start and end apart: 5, of which 4 were waited for; matrix products, arithmetic and copies ran while one was open for 3% of the time, Pallas kernels for 0%

commit v1 on v0

v1 whole, which is shorter than its diff:
```python
import math

import jax
import jax.numpy as jnp
import ml_dtypes
import numpy as np
from jax import lax
from jax.experimental import pallas as pl
from jax.experimental.pallas import tpu as pltpu
from jax.sharding import Mesh
from jax.sharding import PartitionSpec as P

BLK = 128
NB = 32
CG = 4
KH = 40
IN_ROWS = 2 * CG + 1
OUT_ROWS = 3 * CG
PERIOD = 2 * NB * BLK
VMEM = pl.BlockSpec(memory_space=pltpu.VMEM)
PARAMS = pltpu.CompilerParams(vmem_limit_bytes=40 * 1024 * 1024)


def high_low(table):
    high = table.astype(ml_dtypes.bfloat16)
    low = (table - high.astype(np.float64)).astype(ml_dtypes.bfloat16)
    return high, low


def tables():
    k1 = np.arange(KH)
    used = (k1 <= NB)[:, None]
    block = np.arange(NB)
    angle = 2.0 * np.pi * ((k1[:, None] * block[None, :]) % (2 * NB)) / (2 * NB)
    mix = np.concatenate([np.cos(angle) * used, -np.sin(angle) * used], 0)
    high, low = high_low(mix)
    forward_mix = np.concatenate([high, high, low], 1)
    weight = np.where((k1 == 0) | (k1 == NB), 1.0, 2.0)[:, None] * used / PERIOD
    back = np.concatenate([np.cos(angle) * weight, -np.sin(angle) * weight], 0).T
    high, low = high_low(back)
    inverse_mix = np.concatenate([high, high, low], 1)
    offset = np.arange(BLK)
    turn = 2.0 * np.pi * (k1[:, None] * offset[None, :]) / PERIOD
    cos_turn = (np.cos(turn) * used).astype(np.float32)
    sin_turn = (np.sin(turn) * used).astype(np.float32)
    full = 2.0 * np.pi * ((offset[:, None] * offset[None, :]) % BLK) / BLK
    cos, sin = np.cos(full), np.sin(full)
    high, low = high_low(np.block([[cos, -sin], [sin, cos]]))
    forward_full = np.concatenate([high, high, low], 0)
    high, low = high_low(np.block([[cos, sin], [-sin, cos]]))
    inverse_full = np.concatenate([high, high, low], 0)
    return forward_mix, inverse_mix, cos_turn, sin_turn, forward_full, inverse_full


def split(value):
    high = value.astype(jnp.bfloat16)
    low = (value - high.astype(jnp.float32)).astype(jnp.bfloat16)
    return high, low


def dot(left, right):
    return jnp.dot(left, right, preferred_element_type=jnp.float32)


def mix_rows(table, operand):
    high, low = split(operand)
    return dot(table, jnp.concatenate([high, low, high], 0))


def full_transform(operand, table_ref):
    high, low = split(operand)
    return dot(jnp.concatenate([high, low, high], 1), table_ref[...])


def spectra(blocks, mix, cos_turn, sin_turn, full_ref):
    mixed = mix_rows(mix, jnp.concatenate(blocks, 1))
    turned = []
    for index in range(len(blocks)):
        lanes = slice(index * BLK, (index + 1) * BLK)
        real, imag = mixed[:KH, lanes], mixed[KH:, lanes]
        turned.append(
            jnp.concatenate(
                [real * cos_turn + imag * sin_turn, imag * cos_turn - real * sin_turn], 1
            )
        )
    return full_transform(jnp.concatenate(turned, 0), full_ref)


def positions(spectrum, count, mix, cos_turn, sin_turn, full_ref):
    back = full_transform(spectrum, full_ref)
    columns = []
    for index in range(count):
        rows = slice(index * KH, (index + 1) * KH)
        real, imag = back[rows, :BLK], back[rows, BLK:]
        columns.append(
            jnp.concatenate(
                [real * cos_turn - imag * sin_turn, imag * cos_turn + real * sin_turn], 0
            )
        )
    return mix_rows(mix, jnp.concatenate(columns, 1))


def send_kernel(query_ref, key_ref, value_ref, grad_ref, taps_ref, out_ref):
    group = lax.axis_index("zl")
    for part in range(CG):
        lanes = slice(part * BLK, (part + 1) * BLK)
        gated = key_ref[0, :, lanes].astype(jnp.float32) * value_ref[0, :, lanes].astype(jnp.float32)
        grad_s = grad_ref[0, :, lanes].astype(jnp.float32) * query_ref[0, :, lanes].astype(jnp.float32)
        out_ref[pl.ds(part, BLK, IN_ROWS), :] = gated.T
        out_ref[pl.ds(CG + part, BLK, IN_ROWS), :] = grad_s.T
    own = taps_ref[:, pl.ds(pl.multiple_of(group * BLK, BLK), BLK)]
    out_ref[pl.ds(2 * CG, BLK, IN_ROWS), :] = own.T


def forward_kernel(
    rows_ref, mix_ref, cos_ref, sin_ref, full_ref, inv_mix_ref, inv_full_ref, conv_ref, back_ref, lag_ref
):
    mix, cos_turn, sin_turn = mix_ref[...], cos_ref[...], sin_ref[...]
    wide = CG * KH

    def block(seq, row):
        return rows_ref[pl.ds(seq * NB * IN_ROWS + row, NB, IN_ROWS), :]

    taps = spectra([block(part, 2 * CG) for part in range(CG)], mix, cos_turn, sin_turn, full_ref)
    taps_re, taps_im = taps[:, :BLK], taps[:, BLK:]
    lag = None
    for seq in range(CG):
        both = spectra([block(seq, row) for row in range(2 * CG)], mix, cos_turn, sin_turn, full_ref)
        gated_re, gated_im = both[:wide, :BLK], both[:wide, BLK:]
        grad_re, grad_im = both[wide:, :BLK], both[wide:, BLK:]
        rows = slice(seq * wide, (seq + 1) * wide)
        conv_ref[rows, :BLK] = taps_re * gated_re - taps_im * gated_im
        conv_ref[rows, BLK:] = taps_re * gated_im + taps_im * gated_re
        back_ref[rows, :BLK] = taps_re * grad_re + taps_im * grad_im
        back_ref[rows, BLK:] = taps_re * grad_im - taps_im * grad_re
        term = jnp.concatenate(
            [grad_re * gated_re + grad_im * gated_im, grad_im * gated_re - grad_re * gated_im], 1
        )
        lag = term if lag is None else lag + term
    timed = positions(lag, CG, inv_mix_ref[...], cos_turn, sin_turn, inv_full_ref)
    for copy in range(4):
        for part in range(CG):
            first = (copy * CG + part) * NB
            lag_ref[first : first + NB, :] = timed[:, part * BLK : (part + 1) * BLK]


def inverse_kernel(conv_ref, back_ref, cos_ref, sin_ref, mix_ref, full_ref, out_ref):
    mix, cos_turn, sin_turn = mix_ref[...], cos_ref[...], sin_ref[...]
    wide = CG * KH
    for seq in range(CG):
        rows = slice(seq * wide, (seq + 1) * wide)
        for which, ref in enumerate((conv_ref, back_ref)):
            timed = positions(ref[rows, :], CG, mix, cos_turn, sin_turn, full_ref)
            for part in range(CG):
                first = seq * NB * OUT_ROWS + which * CG + part
                out_ref[pl.ds(first, NB, OUT_ROWS), :] = timed[:, part * BLK : (part + 1) * BLK]


def lag_kernel(parts_ref, held_ref, out_ref):
    del held_ref
    own = CG * NB
    total = parts_ref[:own, :] + parts_ref[own : 2 * own, :]
    total = total + (parts_ref[2 * own : 3 * own, :] + parts_ref[3 * own :, :])
    for seq in range(CG):
        for part in range(CG):
            first = seq * NB * OUT_ROWS + 2 * CG + part
            out_ref[pl.ds(first, NB, OUT_ROWS), :] = total[part * NB : (part + 1) * NB, :]


def finish_kernel(
    scale, rows_ref, query_ref, key_ref, value_ref, grad_ref, conv_out_ref, gq_ref, gk_ref, gv_ref, gf_ref
):
    for part in range(CG):
        lanes = slice(part * BLK, (part + 1) * BLK)
        conv_s = rows_ref[pl.ds(part, BLK, OUT_ROWS), :].T
        grad_z = rows_ref[pl.ds(CG + part, BLK, OUT_ROWS), :].T
        lag = rows_ref[pl.ds(2 * CG + part, BLK, OUT_ROWS), :].T
        conv_out_ref[0, :, lanes] = (query_ref[0, :, lanes].astype(jnp.float32) * conv_s).astype(jnp.bfloat16)
        gq_ref[0, :, lanes] = (grad_ref[0, :, lanes].astype(jnp.float32) * conv_s).astype(jnp.bfloat16)
        gk_ref[0, :, lanes] = (grad_z * value_ref[0, :, lanes].astype(jnp.float32)).astype(jnp.bfloat16)
        gv_ref[0, :, lanes] = (grad_z * key_ref[0, :, lanes].astype(jnp.float32)).astype(jnp.bfloat16)
        gf_ref[:, lanes] = lag * scale


def call(kernel, out_shape, count, **kwargs):
    single = not isinstance(out_shape, (tuple, list))
    return pl.pallas_call(
        kernel,
        out_shape=out_shape,
        in_specs=[VMEM] * count,
        out_specs=VMEM if single else [VMEM] * len(out_shape),
        compiler_params=PARAMS,
        **kwargs,
    )


def f32(*shape):
    return jax.ShapeDtypeStruct(shape, jnp.float32)


def exchange(rows, per):
    peers = 4 * NB
    moved = lax.all_to_all(rows.reshape(peers, per, 1, BLK), ("zl", "ctx"), 0, 0, tiled=True)
    return moved.reshape(peers * per, BLK)


def local(queries, keys, values, grad_out, filter_taps):
    forward_mix, inverse_mix, cos_turn, sin_turn, forward_full, inverse_full = (
        jnp.asarray(t) for t in tables()
    )
    sent = call(send_kernel, f32(4 * NB * IN_ROWS, BLK), 5)(queries, keys, values, grad_out, filter_taps)
    rows = exchange(sent, IN_ROWS)
    wide = CG * CG * KH
    conv, back, lag = call(forward_kernel, (f32(wide, 2 * BLK), f32(wide, 2 * BLK), f32(4 * CG * NB, BLK)), 7)(
        rows, forward_mix, cos_turn, sin_turn, forward_full, inverse_mix, inverse_full
    )
    parts = lax.all_to_all(lag.reshape(4, CG * NB, BLK), "y", 0, 0, tiled=True).reshape(4 * CG * NB, BLK)
    timed = call(inverse_kernel, f32(4 * NB * OUT_ROWS, BLK), 6)(
        conv, back, cos_turn, sin_turn, inverse_mix, inverse_full
    )
    timed = call(lag_kernel, f32(4 * NB * OUT_ROWS, BLK), 2, input_output_aliases={1: 0})(parts, timed)
    returned = exchange(timed, OUT_ROWS)
    scale = 1.0 / math.sqrt(16 * NB * BLK)
    shape = jax.ShapeDtypeStruct(queries.shape, jnp.bfloat16)

    def finish(*refs):
        finish_kernel(scale, *refs)

    return tuple(
        call(finish, (shape, shape, shape, shape, f32(*filter_taps.shape)), 5)(
            returned, queries, keys, values, grad_out
        )
    )


def solution(mesh):
    split_mesh = Mesh(mesh.devices.reshape(4, 4, 32), ("y", "zl", "ctx"))
    whole = P(("y", "zl"), "ctx", None)
    return jax.shard_map(
        local,
        mesh=split_mesh,
        in_specs=(whole, whole, whole, whole, P("ctx", None)),
        out_specs=(whole, whole, whole, whole, P("ctx", None)),
        check_vma=False,
    )
```

time: 686 us -> 127 us (0.19)
  the two profiles are of different devices: /device:TPU:2 before, /device:TPU:32 now
where the time goes in v1:
time: 127 us; the launch traced here: 126 us
  blocking collectives  106 us (83%)
  Pallas kernels  5.73 us (5%)
  local copies, waits for them, and re-layouts  4.63 us (4%)
  waiting for transfers between devices  4.6 us (4%)
  starting transfers between devices  4.46 us (4%)
    all_to_all x2, blocking collectives, exchange(): lax.all_to_all(rows.reshape(peers, per, 1, BLK), ('zl', 'ctx'), 0, 0, til...  106 us
    unnamed x30, local copies, waits for them, and re-layouts  4.63 us
    all_to_all x1, waiting for transfers between devices, local(): lax.all_to_all(lag.reshape(4, CG * NB, BLK), 'y', 0, 0, tiled=True)  4.6 us
    all_to_all x1, starting transfers between devices, local(): lax.all_to_all(lag.reshape(4, CG * NB, BLK), 'y', 0, 0, tiled=True)  4.46 us
  transfers between devices with their start and end apart: 1, of which 1 were waited for; matrix products, arithmetic and copies ran while one was open for 0% of the time, Pallas kernels for 2%

profile of v1, /device:TPU:32, one launch (start us, length us, event | category | flops | bytes accessed | tf_op | source)
XLA Modules:
  0.0 126.4 jit_solution(7130435320395240055)
XLA Ops:
  0.6 0.0 copy-start.1
  0.6 0.9 copy-done.1
  1.5 0.9 copy-done.3
  2.4 0.9 copy-done.5
  3.4 0.9 copy-done.7
  4.3 0.9 copy-done.10
  5.2 0.2 shard_map.146
  5.4 0.0 copy-start
  5.4 0.0 copy-start.9
  5.5 0.0 copy-start.11
  5.5 0.0 copy-start.12
  5.5 0.0 copy-start.13
  5.5 0.0 copy-start.14
  5.5 55.2 %all_to_all.15 = f32[128,9,1,128]{3,2,1,0:T(1,128)S(1)} all-to-all(f32[128,9,1,128]{3,2,1,0:T(1,128)S(1)} %bitcast.9), channel_id=1, replica_groups=mesh['y'=4,'zl'=4,'ctx'=32] {'zl','ctx'}, dimensions={0} | all-to-all | bytes 1179648 | tf_op jit(solution)/shard_map/all_to_all | solution.py:203
  60.8 0.0 copy-done
  60.8 0.0 copy-done.9
  60.8 0.0 copy-done.11
  60.8 0.0 copy-done.12
  60.8 0.0 copy-done.13
  60.8 0.0 copy-done.14
  60.8 2.3 %shard_map.147 = (f32[640,256]{1,0:T(8,128)S(1)}, f32[640,256]{1,0:T(8,128)S(1)}, f32[512,128]{1,0:T(8,128)}) custom-call(f32[1152,128]{1,0:T(8,128)S(1)} %bitcast.8, bf16[80,96]{1,0:T(8,128)(2,1)S(1)} %copy-done.14, f32[40,128]{1,0:T(8,128)S(1)} %copy-done.12, f32[40,128]{1,0:T(8,128)S(1)} %copy-done.11, bf16[768,256]{1,0:T(8,128)(2,1)S(1)} %copy-done.9, ...), custom_call_target="tpu_custom_call" | custom-call | tf_op jit(solution)/shard_map/pallas_call | solution.py:214
  63.1 4.5 %all-to-all-start.1 = ((f32[4,128,128]{2,1,0:T(8,128)}), f32[4,128,128]{2,1,0:T(8,128)S(1)}, u32[]{:S(2)}, u32[]{:S(2)}) async-start(f32[4,128,128]{2,1,0:T(8,128)} %bitcast.2), calls=%async_computation.1 | async-start | bytes 524288 | tf_op jit(solution)/shard_map/all_to_all | solution.py:217
  67.5 2.1 %shard_map.148.held_ref = f32[1536,128]{1,0:T(8,128)S(1)} custom-call(f32[640,256]{1,0:T(8,128)S(1)} %get-tuple-element.9.conv_ref, f32[640,256]{1,0:T(8,128)S(1)} %get-tuple-element.10.back_ref, f32[40,128]{1,0:T(8,128)S(1)} %copy-done.12, f32[40,128]{1,0:T(8,128)S(1)} %copy-done.11, bf16[32,240]{1,0:T(8,128)(2,1)S(1)} %copy-done.13, ...), custom_call_target="tpu_custom_call" | custom-call | tf_op jit(solution)/shard_map/pallas_call | solution.py:218
  69.6 4.6 %all-to-all-done.1 = f32[4,128,128]{2,1,0:T(8,128)S(1)} async-done(((f32[4,128,128]{2,1,0:T(8,128)}), f32[4,128,128]{2,1,0:T(8,128)S(1)}, u32[]{:S(2)}, u32[]{:S(2)}) %all-to-all-start.1) | async-done | bytes 262176 | tf_op jit(solution)/shard_map/all_to_all | solution.py:217
  74.3 0.0 copy-start.2
  74.3 0.0 copy-start.4
  74.3 0.0 copy-start.6
  74.3 0.0 copy-start.8
  74.3 50.9 %all_to_all.16 = f32[128,12,1,128]{3,2,1,0:T(1,128)S(1)} all-to-all(f32[128,12,1,128]{3,2,1,0:T(1,128)S(1)} %bitcast.6), channel_id=1, replica_groups=mesh['y'=4,'zl'=4,'ctx'=32] {'zl','ctx'}, dimensions={0} | all-to-all | bytes 1572864 | tf_op jit(solution)/shard_map/all_to_all | solution.py:203
  125.2 0.0 copy-done.2
  125.2 0.0 copy-done.4
  125.3 1.1 shard_map.150
  (7 shorter events, 0.0 us)
Async XLA Ops:
  0.6 0.9 copy-start.1
  1.5 0.9 copy-start.3
  2.4 0.9 copy-start.5
  3.3 0.9 copy-start.7
  4.3 0.9 copy-start.10
  5.4 55.3 %copy-start = (bf16[768,256]{1,0:T(8,128)(2,1)S(1)}, bf16[768,256]{1,0:T(8,128)(2,1)}, u32[]{:S(2)}) copy-start(bf16[768,256]{1,0:T(8,128)(2,1)} %constant.17.clone.inv_full_ref.full_ref) | copy-start | bytes 1179652
  5.4 55.3 %copy-start.9 = (bf16[768,256]{1,0:T(8,128)(2,1)S(1)}, bf16[768,256]{1,0:T(8,128)(2,1)}, u32[]{:S(2)}) copy-start(bf16[768,256]{1,0:T(8,128)(2,1)} %constant.16.clone.full_ref) | copy-start | bytes 1179652
  5.5 55.3 %copy-start.11 = (f32[40,128]{1,0:T(8,128)S(1)}, f32[40,128]{1,0:T(8,128)}, u32[]{:S(2)}) copy-start(f32[40,128]{1,0:T(8,128)} %constant.15.clone.sin_ref) | copy-start | bytes 61444
  5.5 55.3 %copy-start.12 = (f32[40,128]{1,0:T(8,128)S(1)}, f32[40,128]{1,0:T(8,128)}, u32[]{:S(2)}) copy-start(f32[40,128]{1,0:T(8,128)} %constant.14.clone.cos_ref) | copy-start | bytes 61444
  5.5 55.3 %copy-start.13 = (bf16[32,240]{1,0:T(8,128)(2,1)S(1)}, bf16[32,240]{1,0:T(8,128)(2,1)}, u32[]{:S(2)}) copy-start(bf16[32,240]{1,0:T(8,128)(2,1)} %constant.13.clone.inv_mix_ref.mix_ref) | copy-start | bytes 46084
  5.5 55.3 %copy-start.14 = (bf16[80,96]{1,0:T(8,128)(2,1)S(1)}, bf16[80,96]{1,0:T(8,128)(2,1)}, u32[]{:S(2)}) copy-start(bf16[80,96]{1,0:T(8,128)(2,1)} %constant.12.clone.mix_ref) | copy-start | bytes 46084
  63.1 11.1 %all-to-all-start.1 = ((f32[4,128,128]{2,1,0:T(8,128)}), f32[4,128,128]{2,1,0:T(8,128)S(1)}, u32[]{:S(2)}, u32[]{:S(2)}) async-start(f32[4,128,128]{2,1,0:T(8,128)} %bitcast.2), calls=%async_computation.1 | async-start | bytes 524288 | tf_op jit(solution)/shard_map/all_to_all | solution.py:217
  74.3 51.0 %copy-start.2 = (bf16[1,128,512]{2,1,0:T(8,128)(2,1)S(1)}, bf16[1,128,512]{2,1,0:T(8,128)(2,1)}, u32[]{:S(2)}) copy-start(bf16[1,128,512]{2,1,0:T(8,128)(2,1)} %refs_1_.1) | copy-start | bytes 393220
  74.3 51.0 %copy-start.4 = (bf16[1,128,512]{2,1,0:T(8,128)(2,1)S(1)}, bf16[1,128,512]{2,1,0:T(8,128)(2,1)}, u32[]{:S(2)}) copy-start(bf16[1,128,512]{2,1,0:T(8,128)(2,1)} %refs_2_.1) | copy-start | bytes 393220
  74.3 51.0 %copy-start.6 = (bf16[1,128,512]{2,1,0:T(8,128)(2,1)S(1)}, bf16[1,128,512]{2,1,0:T(8,128)(2,1)}, u32[]{:S(2)}) copy-start(bf16[1,128,512]{2,1,0:T(8,128)(2,1)} %refs_3_.1) | copy-start | bytes 393220
  74.3 51.0 %copy-start.8 = (bf16[1,128,512]{2,1,0:T(8,128)(2,1)S(1)}, bf16[1,128,512]{2,1,0:T(8,128)(2,1)}, u32[]{:S(2)}) copy-start(bf16[1,128,512]{2,1,0:T(8,128)(2,1)} %refs_4_.1) | copy-start | bytes 393220

commit v2 on v1

--- a/solution.py
+++ b/solution.py
@@ -18,6 +18,7 @@
 OUT_ROWS = 3 * CG
 PERIOD = 2 * NB * BLK
 VMEM = pl.BlockSpec(memory_space=pltpu.VMEM)
+HBM = pl.BlockSpec(memory_space=pltpu.HBM)
 PARAMS = pltpu.CompilerParams(vmem_limit_bytes=40 * 1024 * 1024)
 
 
@@ -100,39 +101,47 @@
     return mix_rows(mix, jnp.concatenate(columns, 1))
 
 
-def send_kernel(query_ref, key_ref, value_ref, grad_ref, taps_ref, out_ref):
+def send_kernel(query_ref, key_ref, value_ref, grad_ref, taps_ref, out_ref, query, key, value, grad, taps, sems):
     group = lax.axis_index("zl")
+    own = taps_ref.at[:, pl.ds(pl.multiple_of(group * BLK, BLK), BLK)]
+    pairs = ((key_ref, key), (value_ref, value), (grad_ref, grad), (query_ref, query), (own, taps))
+    copies = [pltpu.make_async_copy(src, dst, sems.at[index]) for index, (src, dst) in enumerate(pairs)]
+    for copy in copies:
+        copy.start()
+    copies[0].wait()
+    copies[1].wait()
     for part in range(CG):
         lanes = slice(part * BLK, (part + 1) * BLK)
-        gated = key_ref[0, :, lanes].astype(jnp.float32) * value_ref[0, :, lanes].astype(jnp.float32)
-        grad_s = grad_ref[0, :, lanes].astype(jnp.float32) * query_ref[0, :, lanes].astype(jnp.float32)
+        gated = key[0, :, lanes].astype(jnp.float32) * value[0, :, lanes].astype(jnp.float32)
         out_ref[pl.ds(part, BLK, IN_ROWS), :] = gated.T
+    copies[2].wait()
+    copies[3].wait()
+    for part in range(CG):
+        lanes = slice(part * BLK, (part + 1) * BLK)
+        grad_s = grad[0, :, lanes].astype(jnp.float32) * query[0, :, lanes].astype(jnp.float32)
         out_ref[pl.ds(CG + part, BLK, IN_ROWS), :] = grad_s.T
-    own = taps_ref[:, pl.ds(pl.multiple_of(group * BLK, BLK), BLK)]
-    out_ref[pl.ds(2 * CG, BLK, IN_ROWS), :] = own.T
+    copies[4].wait()
+    out_ref[pl.ds(2 * CG, BLK, IN_ROWS), :] = taps[...].T
+
+
+def block(rows_ref, seq, row):
+    return rows_ref[pl.ds(seq * NB * IN_ROWS + row, NB, IN_ROWS), :]
 
 
 def forward_kernel(
-    rows_ref, mix_ref, cos_ref, sin_ref, full_ref, inv_mix_ref, inv_full_ref, conv_ref, back_ref, lag_ref
+    rows_ref, mix_ref, cos_ref, sin_ref, full_ref, inv_mix_ref, inv_full_ref, gated_ref, grad_ref, lag_ref
 ):
     mix, cos_turn, sin_turn = mix_ref[...], cos_ref[...], sin_ref[...]
     wide = CG * KH
-
-    def block(seq, row):
-        return rows_ref[pl.ds(seq * NB * IN_ROWS + row, NB, IN_ROWS), :]
-
-    taps = spectra([block(part, 2 * CG) for part in range(CG)], mix, cos_turn, sin_turn, full_ref)
-    taps_re, taps_im = taps[:, :BLK], taps[:, BLK:]
     lag = None
     for seq in range(CG):
-        both = spectra([block(seq, row) for row in range(2 * CG)], mix, cos_turn, sin_turn, full_ref)
+        blocks = [block(rows_ref, seq, row) for row in range(2 * CG)]
+        both = spectra(blocks, mix, cos_turn, sin_turn, full_ref)
+        rows = slice(seq * wide, (seq + 1) * wide)
+        gated_ref[rows, :] = both[:wide]
+        grad_ref[rows, :] = both[wide:]
         gated_re, gated_im = both[:wide, :BLK], both[:wide, BLK:]
         grad_re, grad_im = both[wide:, :BLK], both[wide:, BLK:]
-        rows = slice(seq * wide, (seq + 1) * wide)
-        conv_ref[rows, :BLK] = taps_re * gated_re - taps_im * gated_im
-        conv_ref[rows, BLK:] = taps_re * gated_im + taps_im * gated_re
-        back_ref[rows, :BLK] = taps_re * grad_re + taps_im * grad_im
-        back_ref[rows, BLK:] = taps_re * grad_im - taps_im * grad_re
         term = jnp.concatenate(
             [grad_re * gated_re + grad_im * gated_im, grad_im * gated_re - grad_re * gated_im], 1
         )
@@ -144,27 +153,39 @@
             lag_ref[first : first + NB, :] = timed[:, part * BLK : (part + 1) * BLK]
 
 
-def inverse_kernel(conv_ref, back_ref, cos_ref, sin_ref, mix_ref, full_ref, out_ref):
+def inverse_kernel(
+    rows_ref, gated_ref, grad_ref, mix_ref, cos_ref, sin_ref, full_ref, inv_mix_ref, inv_full_ref, out_ref
+):
     mix, cos_turn, sin_turn = mix_ref[...], cos_ref[...], sin_ref[...]
+    inv_mix = inv_mix_ref[...]
     wide = CG * KH
+    taps = spectra([block(rows_ref, part, 2 * CG) for part in range(CG)], mix, cos_turn, sin_turn, full_ref)
+    taps_re, taps_im = taps[:, :BLK], taps[:, BLK:]
     for seq in range(CG):
         rows = slice(seq * wide, (seq + 1) * wide)
-        for which, ref in enumerate((conv_ref, back_ref)):
-            timed = positions(ref[rows, :], CG, mix, cos_turn, sin_turn, full_ref)
-            for part in range(CG):
-                first = seq * NB * OUT_ROWS + which * CG + part
-                out_ref[pl.ds(first, NB, OUT_ROWS), :] = timed[:, part * BLK : (part + 1) * BLK]
-
-
-def lag_kernel(parts_ref, held_ref, out_ref):
-    del held_ref
-    own = CG * NB
-    total = parts_ref[:own, :] + parts_ref[own : 2 * own, :]
-    total = total + (parts_ref[2 * own : 3 * own, :] + parts_ref[3 * own :, :])
+        gated_re, gated_im = gated_ref[rows, :BLK], gated_ref[rows, BLK:]
+        grad_re, grad_im = grad_ref[rows, :BLK], grad_ref[rows, BLK:]
+        conv = jnp.concatenate(
+            [taps_re * gated_re - taps_im * gated_im, taps_re * gated_im + taps_im * gated_re], 1
+        )
+        back = jnp.concatenate(
+            [taps_re * grad_re + taps_im * grad_im, taps_re * grad_im - taps_im * grad_re], 1
+        )
+        timed = positions(jnp.concatenate([conv, back], 0), 2 * CG, inv_mix, cos_turn, sin_turn, inv_full_ref)
+        for row in range(2 * CG):
+            out_ref[pl.ds(seq * NB * 2 * CG + row, NB, 2 * CG), :] = timed[:, row * BLK : (row + 1) * BLK]
+
+
+def join_kernel(shares_ref, timed_ref, out_ref):
+    peers = CG * NB
+    lag = shares_ref[:peers, :] + shares_ref[peers : 2 * peers, :]
+    lag = lag + (shares_ref[2 * peers : 3 * peers, :] + shares_ref[3 * peers :, :])
+    for row in range(2 * CG):
+        out_ref[pl.ds(row, peers, OUT_ROWS), :] = timed_ref[pl.ds(row, peers, 2 * CG), :]
     for seq in range(CG):
         for part in range(CG):
             first = seq * NB * OUT_ROWS + 2 * CG + part
-            out_ref[pl.ds(first, NB, OUT_ROWS), :] = total[part * NB : (part + 1) * NB, :]
+            out_ref[pl.ds(first, NB, OUT_ROWS), :] = lag[part * NB : (part + 1) * NB, :]
 
 
 def finish_kernel(
@@ -182,14 +203,14 @@
         gf_ref[:, lanes] = lag * scale
 
 
-def call(kernel, out_shape, count, **kwargs):
+def call(kernel, out_shape, count, space=VMEM, params=PARAMS, **kwargs):
     single = not isinstance(out_shape, (tuple, list))
     return pl.pallas_call(
         kernel,
         out_shape=out_shape,
-        in_specs=[VMEM] * count,
+        in_specs=[space] * count,
         out_specs=VMEM if single else [VMEM] * len(out_shape),
-        compiler_params=PARAMS,
+        compiler_params=params,
         **kwargs,
     )
 
@@ -199,7 +220,7 @@
 
 
 def exchange(rows, per):
-    peers = 4 * NB
+    peers = CG * NB
     moved = lax.all_to_all(rows.reshape(peers, per, 1, BLK), ("zl", "ctx"), 0, 0, tiled=True)
     return moved.reshape(peers * per, BLK)
 
@@ -208,18 +229,25 @@
     forward_mix, inverse_mix, cos_turn, sin_turn, forward_full, inverse_full = (
         jnp.asarray(t) for t in tables()
     )
-    sent = call(send_kernel, f32(4 * NB * IN_ROWS, BLK), 5)(queries, keys, values, grad_out, filter_taps)
+    peers = CG * NB
+    wide = CG * CG * KH
+    scratch = [pltpu.VMEM(queries.shape, jnp.bfloat16)] * 4 + [
+        pltpu.VMEM((BLK, BLK), jnp.float32),
+        pltpu.SemaphoreType.DMA((5,)),
+    ]
+    sent = call(send_kernel, f32(peers * IN_ROWS, BLK), 5, HBM, None, scratch_shapes=scratch)(
+        queries, keys, values, grad_out, filter_taps
+    )
     rows = exchange(sent, IN_ROWS)
-    wide = CG * CG * KH
-    conv, back, lag = call(forward_kernel, (f32(wide, 2 * BLK), f32(wide, 2 * BLK), f32(4 * CG * NB, BLK)), 7)(
+    gated, grad, lag = call(forward_kernel, (f32(wide, 2 * BLK), f32(wide, 2 * BLK), f32(4 * peers, BLK)), 7)(
         rows, forward_mix, cos_turn, sin_turn, forward_full, inverse_mix, inverse_full
     )
-    parts = lax.all_to_all(lag.reshape(4, CG * NB, BLK), "y", 0, 0, tiled=True).reshape(4 * CG * NB, BLK)
-    timed = call(inverse_kernel, f32(4 * NB * OUT_ROWS, BLK), 6)(
-        conv, back, cos_turn, sin_turn, inverse_mix, inverse_full
-    )
-    timed = call(lag_kernel, f32(4 * NB * OUT_ROWS, BLK), 2, input_output_aliases={1: 0})(parts, timed)
-    returned = exchange(timed, OUT_ROWS)
+    shares = lax.all_to_all(lag.reshape(4, peers, BLK), "y", 0, 0, tiled=True).reshape(4 * peers, BLK)
+    timed = call(inverse_kernel, f32(peers * 2 * CG, BLK), 9)(
+        rows, gated, grad, forward_mix, cos_turn, sin_turn, forward_full, inverse_mix, inverse_full
+    )
+    joined = call(join_kernel, f32(peers * OUT_ROWS, BLK), 2)(shares, timed)
+    returned = exchange(joined, OUT_ROWS)
     scale = 1.0 / math.sqrt(16 * NB * BLK)
     shape = jax.ShapeDtypeStruct(queries.shape, jnp.bfloat16)
 

time: 127 us -> 124 us (0.976)
  local copies, waits for them, and re-layouts: 4.63 us -> 0.07 us
  Pallas kernels: 5.73 us -> 7.48 us
    unnamed x30 -> x20, local copies, waits for them, and re-layouts: 4.63 us -> 0.07 us
    pallas_call x4, Pallas kernels: 4.61 us -> 6.37 us  [the longest x1 2.21 us: local(): call(send_kernel, f32(peers * IN_ROWS, BLK), 5, HBM, None, scratch_shapes...]
where the time goes in v2:
time: 124 us
  blocking collectives  106 us (85%)
  Pallas kernels  7.48 us (6%)
  waiting for transfers between devices  4.75 us (4%)
  starting transfers between devices  4.46 us (4%)
    all_to_all x2, blocking collectives, exchange(): lax.all_to_all(rows.reshape(peers, per, 1, BLK), ('zl', 'ctx'), 0, 0, til...  106 us
    all_to_all x1, waiting for transfers between devices, local(): lax.all_to_all(lag.reshape(4, peers, BLK), 'y', 0, 0, tiled=True)  4.75 us
    all_to_all x1, starting transfers between devices, local(): lax.all_to_all(lag.reshape(4, peers, BLK), 'y', 0, 0, tiled=True)  4.46 us
  transfers between devices with their start and end apart: 1, of which 1 were waited for; matrix products, arithmetic and copies ran while one was open for 0% of the time, Pallas kernels for 2%

profile of v2, /device:TPU:32, one launch (start us, length us, event | category | flops | bytes accessed | tf_op | source)
XLA Modules:
  0.0 123.9 jit_solution(17335721622119825435)
XLA Ops:
  0.6 2.2 %shard_map.146 = f32[1152,128]{1,0:T(8,128)} custom-call(bf16[1,128,512]{2,1,0:T(8,128)(2,1)} %refs_1_.1, bf16[1,128,512]{2,1,0:T(8,128)(2,1)} %refs_2_.1, bf16[1,128,512]{2,1,0:T(8,128)(2,1)} %refs_3_.1, bf16[1,128,512]{2,1,0:T(8,128)(2,1)} %refs_4_.1, f32[128,512]{1,0:T(8,128)} %taps_ref.1), custom_call_target="tpu_custom_call" | custom-call | tf_op jit(solution)/shard_map/pallas_call | solution.py:238
  2.9 0.0 copy-start
  2.9 0.0 copy-start.1
  2.9 0.0 copy-start.6
  2.9 0.0 copy-start.7
  2.9 0.0 copy-start.8
  2.9 0.0 copy-start.9
  2.9 55.5 %all_to_all.15 = f32[128,9,1,128]{3,2,1,0:T(1,128)S(1)} all-to-all(f32[128,9,1,128]{3,2,1,0:T(1,128)} %bitcast.11), channel_id=1, replica_groups=mesh['y'=4,'zl'=4,'ctx'=32] {'zl','ctx'}, dimensions={0} | all-to-all | bytes 1179648 | tf_op jit(solution)/shard_map/all_to_all | solution.py:224
  58.4 0.0 copy-done
  58.4 0.0 copy-done.1
  58.4 0.0 copy-done.6
  58.4 0.0 copy-done.7
  58.4 0.0 copy-done.8
  58.4 0.0 copy-done.9
  58.4 2.1 %shard_map.147 = (f32[640,256]{1,0:T(8,128)S(1)}, f32[640,256]{1,0:T(8,128)S(1)}, f32[512,128]{1,0:T(8,128)}) custom-call(f32[1152,128]{1,0:T(8,128)S(1)} %bitcast.6, bf16[80,96]{1,0:T(8,128)(2,1)S(1)} %copy-done.6, f32[40,128]{1,0:T(8,128)S(1)} %copy-done.7, f32[40,128]{1,0:T(8,128)S(1)} %copy-done.8, bf16[768,256]{1,0:T(8,128)(2,1)S(1)} %copy-done, ...), custom_call_target="tpu_custom_call" | custom-call | tf_op jit(solution)/shard_map/pallas_call | solution.py:242
  60.5 4.5 %all-to-all-start.1 = ((f32[4,128,128]{2,1,0:T(8,128)}), f32[4,128,128]{2,1,0:T(8,128)S(1)}, u32[]{:S(2)}, u32[]{:S(2)}) async-start(f32[4,128,128]{2,1,0:T(8,128)} %bitcast.2), calls=%async_computation.1 | async-start | bytes 524288 | tf_op jit(solution)/shard_map/all_to_all | solution.py:245
  65.0 1.9 %shard_map.148.timed_ref = f32[1024,128]{1,0:T(8,128)S(1)} custom-call(f32[1152,128]{1,0:T(8,128)S(1)} %bitcast.7, f32[640,256]{1,0:T(8,128)S(1)} %get-tuple-element.9.gated_ref, f32[640,256]{1,0:T(8,128)S(1)} %get-tuple-element.10.grad_ref, bf16[80,96]{1,0:T(8,128)(2,1)S(1)} %copy-done.6, f32[40,128]{1,0:T(8,128)S(1)} %copy-done.7, ...), custom_call_target="tpu_custom_call" | custom-call | tf_op jit(solution)/shard_map/pallas_call | solution.py:246
  66.9 4.7 %all-to-all-done.1 = f32[4,128,128]{2,1,0:T(8,128)S(1)} async-done(((f32[4,128,128]{2,1,0:T(8,128)}), f32[4,128,128]{2,1,0:T(8,128)S(1)}, u32[]{:S(2)}, u32[]{:S(2)}) %all-to-all-start.1) | async-done | bytes 262176 | tf_op jit(solution)/shard_map/all_to_all | solution.py:245
  71.7 0.1 shard_map.149
  71.8 0.0 copy-start.2
  71.8 0.0 copy-start.3
  71.8 0.0 copy-start.4
  71.8 0.0 copy-start.5
  71.8 50.9 %all_to_all.16 = f32[128,12,1,128]{3,2,1,0:T(1,128)S(1)} all-to-all(f32[128,12,1,128]{3,2,1,0:T(1,128)S(1)} %bitcast.9), channel_id=1, replica_groups=mesh['y'=4,'zl'=4,'ctx'=32] {'zl','ctx'}, dimensions={0} | all-to-all | bytes 1572864 | tf_op jit(solution)/shard_map/all_to_all | solution.py:224
  122.8 0.0 copy-done.2
  122.8 0.0 copy-done.3
  122.8 0.0 copy-done.4
  122.8 0.0 copy-done.5
  122.8 1.1 shard_map.150
Async XLA Ops:
  2.9 55.5 %copy-start = (bf16[768,256]{1,0:T(8,128)(2,1)S(1)}, bf16[768,256]{1,0:T(8,128)(2,1)}, u32[]{:S(2)}) copy-start(bf16[768,256]{1,0:T(8,128)(2,1)} %constant.16.clone.full_ref) | copy-start | bytes 1179652
  2.9 55.5 %copy-start.1 = (bf16[768,256]{1,0:T(8,128)(2,1)S(1)}, bf16[768,256]{1,0:T(8,128)(2,1)}, u32[]{:S(2)}) copy-start(bf16[768,256]{1,0:T(8,128)(2,1)} %constant.17.clone.inv_full_ref) | copy-start | bytes 1179652
  2.9 55.5 %copy-start.6 = (bf16[80,96]{1,0:T(8,128)(2,1)S(1)}, bf16[80,96]{1,0:T(8,128)(2,1)}, u32[]{:S(2)}) copy-start(bf16[80,96]{1,0:T(8,128)(2,1)} %constant.12.clone.mix_ref) | copy-start | bytes 46084
  2.9 55.5 %copy-start.7 = (f32[40,128]{1,0:T(8,128)S(1)}, f32[40,128]{1,0:T(8,128)}, u32[]{:S(2)}) copy-start(f32[40,128]{1,0:T(8,128)} %constant.14.clone.cos_ref) | copy-start | bytes 61444
  2.9 55.5 %copy-start.8 = (f32[40,128]{1,0:T(8,128)S(1)}, f32[40,128]{1,0:T(8,128)}, u32[]{:S(2)}) copy-start(f32[40,128]{1,0:T(8,128)} %constant.15.clone.sin_ref) | copy-start | bytes 61444
  2.9 55.5 %copy-start.9 = (bf16[32,240]{1,0:T(8,128)(2,1)S(1)}, bf16[32,240]{1,0:T(8,128)(2,1)}, u32[]{:S(2)}) copy-start(bf16[32,240]{1,0:T(8,128)(2,1)} %constant.13.clone.inv_mix_ref) | copy-start | bytes 46084
  60.5 11.1 %all-to-all-start.1 = ((f32[4,128,128]{2,1,0:T(8,128)}), f32[4,128,128]{2,1,0:T(8,128)S(1)}, u32[]{:S(2)}, u32[]{:S(2)}) async-start(f32[4,128,128]{2,1,0:T(8,128)} %bitcast.2), calls=%async_computation.1 | async-start | bytes 524288 | tf_op jit(solution)/shard_map/all_to_all | solution.py:245
  71.8 51.0 %copy-start.2 = (bf16[1,128,512]{2,1,0:T(8,128)(2,1)S(1)}, bf16[1,128,512]{2,1,0:T(8,128)(2,1)}, u32[]{:S(2)}) copy-start(bf16[1,128,512]{2,1,0:T(8,128)(2,1)} %refs_1_.1) | copy-start | bytes 393220
  71.8 51.0 %copy-start.3 = (bf16[1,128,512]{2,1,0:T(8,128)(2,1)S(1)}, bf16[1,128,512]{2,1,0:T(8,128)(2,1)}, u32[]{:S(2)}) copy-start(bf16[1,128,512]{2,1,0:T(8,128)(2,1)} %refs_2_.1) | copy-start | bytes 393220
  71.8 51.0 %copy-start.4 = (bf16[1,128,512]{2,1,0:T(8,128)(2,1)S(1)}, bf16[1,128,512]{2,1,0:T(8,128)(2,1)}, u32[]{:S(2)}) copy-start(bf16[1,128,512]{2,1,0:T(8,128)(2,1)} %refs_3_.1) | copy-start | bytes 393220
  71.8 51.0 %copy-start.5 = (bf16[1,128,512]{2,1,0:T(8,128)(2,1)S(1)}, bf16[1,128,512]{2,1,0:T(8,128)(2,1)}, u32[]{:S(2)}) copy-start(bf16[1,128,512]{2,1,0:T(8,128)(2,1)} %refs_4_.1) | copy-start | bytes 393220

commit v3 on v2

--- a/solution.py
+++ b/solution.py
@@ -1,3 +1,4 @@
+import functools
 import math
 
 import jax
@@ -15,10 +16,11 @@
 CG = 4
 KH = 40
 IN_ROWS = 2 * CG + 1
-OUT_ROWS = 3 * CG
+OUT_ROWS = 2 * CG + 1
 PERIOD = 2 * NB * BLK
 VMEM = pl.BlockSpec(memory_space=pltpu.VMEM)
 HBM = pl.BlockSpec(memory_space=pltpu.HBM)
+SMALL = pltpu.CompilerParams(vmem_limit_bytes=8 * 1024 * 1024)
 PARAMS = pltpu.CompilerParams(vmem_limit_bytes=40 * 1024 * 1024)
 
 
@@ -147,10 +149,8 @@
         )
         lag = term if lag is None else lag + term
     timed = positions(lag, CG, inv_mix_ref[...], cos_turn, sin_turn, inv_full_ref)
-    for copy in range(4):
-        for part in range(CG):
-            first = (copy * CG + part) * NB
-            lag_ref[first : first + NB, :] = timed[:, part * BLK : (part + 1) * BLK]
+    for part in range(CG):
+        lag_ref[part * NB : (part + 1) * NB, :] = timed[:, part * BLK : (part + 1) * BLK]
 
 
 def inverse_kernel(
@@ -178,29 +178,34 @@
 
 def join_kernel(shares_ref, timed_ref, out_ref):
     peers = CG * NB
-    lag = shares_ref[:peers, :] + shares_ref[peers : 2 * peers, :]
-    lag = lag + (shares_ref[2 * peers : 3 * peers, :] + shares_ref[3 * peers :, :])
+    lag = shares_ref[:NB, :] + shares_ref[NB : 2 * NB, :]
+    lag = lag + (shares_ref[2 * NB : 3 * NB, :] + shares_ref[3 * NB :, :])
     for row in range(2 * CG):
         out_ref[pl.ds(row, peers, OUT_ROWS), :] = timed_ref[pl.ds(row, peers, 2 * CG), :]
     for seq in range(CG):
-        for part in range(CG):
-            first = seq * NB * OUT_ROWS + 2 * CG + part
-            out_ref[pl.ds(first, NB, OUT_ROWS), :] = lag[part * NB : (part + 1) * NB, :]
-
-
-def finish_kernel(
-    scale, rows_ref, query_ref, key_ref, value_ref, grad_ref, conv_out_ref, gq_ref, gk_ref, gv_ref, gf_ref
-):
+        out_ref[pl.ds(seq * NB * OUT_ROWS + 2 * CG, NB, OUT_ROWS), :] = lag
+
+
+def share_kernel(scale, rows_ref, out_ref):
+    lag = rows_ref[pl.ds(2 * CG, BLK, OUT_ROWS), :].T * scale
+    for copy in range(CG):
+        out_ref[copy * BLK : (copy + 1) * BLK, :] = lag
+
+
+def finish_kernel(rows_ref, query_ref, key_ref, value_ref, grad_ref, conv_out_ref, gq_ref, gk_ref, gv_ref):
     for part in range(CG):
         lanes = slice(part * BLK, (part + 1) * BLK)
         conv_s = rows_ref[pl.ds(part, BLK, OUT_ROWS), :].T
         grad_z = rows_ref[pl.ds(CG + part, BLK, OUT_ROWS), :].T
-        lag = rows_ref[pl.ds(2 * CG + part, BLK, OUT_ROWS), :].T
         conv_out_ref[0, :, lanes] = (query_ref[0, :, lanes].astype(jnp.float32) * conv_s).astype(jnp.bfloat16)
         gq_ref[0, :, lanes] = (grad_ref[0, :, lanes].astype(jnp.float32) * conv_s).astype(jnp.bfloat16)
         gk_ref[0, :, lanes] = (grad_z * value_ref[0, :, lanes].astype(jnp.float32)).astype(jnp.bfloat16)
         gv_ref[0, :, lanes] = (grad_z * key_ref[0, :, lanes].astype(jnp.float32)).astype(jnp.bfloat16)
-        gf_ref[:, lanes] = lag * scale
+
+
+def spread_kernel(parts_ref, out_ref):
+    for part in range(CG):
+        out_ref[:, part * BLK : (part + 1) * BLK] = parts_ref[part * BLK : (part + 1) * BLK, :]
 
 
 def call(kernel, out_shape, count, space=VMEM, params=PARAMS, **kwargs):
@@ -225,6 +230,11 @@
     return moved.reshape(peers * per, BLK)
 
 
+def across_y(rows):
+    moved = lax.all_to_all(rows.reshape(4, -1, BLK), "y", 0, 0, tiled=True)
+    return moved.reshape(rows.shape)
+
+
 def local(queries, keys, values, grad_out, filter_taps):
     forward_mix, inverse_mix, cos_turn, sin_turn, forward_full, inverse_full = (
         jnp.asarray(t) for t in tables()
@@ -235,30 +245,24 @@
         pltpu.VMEM((BLK, BLK), jnp.float32),
         pltpu.SemaphoreType.DMA((5,)),
     ]
-    sent = call(send_kernel, f32(peers * IN_ROWS, BLK), 5, HBM, None, scratch_shapes=scratch)(
-        queries, keys, values, grad_out, filter_taps
+    sent = call(send_kernel, f32(peers * IN_ROWS, BLK), 5, HBM, SMALL, scratch_shapes=scratch)(
+        *(pltpu.with_memory_space_constraint(a, pltpu.HBM) for a in (queries, keys, values, grad_out, filter_taps))
     )
     rows = exchange(sent, IN_ROWS)
-    gated, grad, lag = call(forward_kernel, (f32(wide, 2 * BLK), f32(wide, 2 * BLK), f32(4 * peers, BLK)), 7)(
+    gated, grad, lag = call(forward_kernel, (f32(wide, 2 * BLK), f32(wide, 2 * BLK), f32(peers, BLK)), 7)(
         rows, forward_mix, cos_turn, sin_turn, forward_full, inverse_mix, inverse_full
     )
-    shares = lax.all_to_all(lag.reshape(4, peers, BLK), "y", 0, 0, tiled=True).reshape(4 * peers, BLK)
+    shares = across_y(lag)
     timed = call(inverse_kernel, f32(peers * 2 * CG, BLK), 9)(
         rows, gated, grad, forward_mix, cos_turn, sin_turn, forward_full, inverse_mix, inverse_full
     )
     joined = call(join_kernel, f32(peers * OUT_ROWS, BLK), 2)(shares, timed)
     returned = exchange(joined, OUT_ROWS)
     scale = 1.0 / math.sqrt(16 * NB * BLK)
+    spread = across_y(call(functools.partial(share_kernel, scale), f32(CG * BLK, BLK), 1)(returned))
     shape = jax.ShapeDtypeStruct(queries.shape, jnp.bfloat16)
-
-    def finish(*refs):
-        finish_kernel(scale, *refs)
-
-    return tuple(
-        call(finish, (shape, shape, shape, shape, f32(*filter_taps.shape)), 5)(
-            returned, queries, keys, values, grad_out
-        )
-    )
+    products = call(finish_kernel, (shape, shape, shape, shape), 5)(returned, queries, keys, values, grad_out)
+    return (*products, call(spread_kernel, f32(*filter_taps.shape), 1)(spread))
 
 
 def solution(mesh):

time: 124 us -> 124 us (level)
  blocking collectives: 106 us -> 97.8 us
  waiting for transfers between devices: 4.75 us -> 9.31 us
  starting transfers between devices: 4.46 us -> 8.01 us
    all_to_all x2, blocking collectives: 106 us -> 97.8 us  [exchange(): lax.all_to_all(rows.reshape(peers, per, 1, BLK), ('zl', 'ctx'), 0, 0, til...]
    all_to_all x1 -> x2, waiting for transfers between devices: 4.75 us -> 9.31 us  [across_y(): moved = lax.all_to_all(rows.reshape(4, -1, BLK), 'y', 0, 0, tiled=True)]
    all_to_all x1 -> x2, starting transfers between devices: 4.46 us -> 8.01 us  [across_y(): moved = lax.all_to_all(rows.reshape(4, -1, BLK), 'y', 0, 0, tiled=True)]
    pallas_call x3 -> x5, Pallas kernels: 5.43 us -> 5.94 us  [the longest x1 2.02 us: local(): call(forward_kernel, (f32(wide, 2 * BLK), f32(wide, 2 * BLK), f32(peers,...]
  transfers between devices with their start and end apart: 1 -> 2, of which waited for: 1 -> 2; matrix products, arithmetic and copies ran while one was open for 0% -> 0% of each run, Pallas kernels for 2% -> 2%
where the time goes in v3:
time: 124 us
  blocking collectives  97.8 us (79%)
  waiting for transfers between devices  9.31 us (8%)
  starting transfers between devices  8.01 us (6%)
  Pallas kernels  7.98 us (6%)
    all_to_all x2, blocking collectives, exchange(): lax.all_to_all(rows.reshape(peers, per, 1, BLK), ('zl', 'ctx'), 0, 0, til...  97.8 us
    all_to_all x2, waiting for transfers between devices, across_y(): moved = lax.all_to_all(rows.reshape(4, -1, BLK), 'y', 0, 0, tiled=True)  9.31 us
    all_to_all x2, starting transfers between devices, across_y(): moved = lax.all_to_all(rows.reshape(4, -1, BLK), 'y', 0, 0, tiled=True)  8.01 us
  transfers between devices with their start and end apart: 2, of which 2 were waited for; matrix products, arithmetic and copies ran while one was open for 0% of the time, Pallas kernels for 2%

profile of v3, /device:TPU:32, one launch (start us, length us, event | category | flops | bytes accessed | tf_op | source)
XLA Modules:
  0.0 123.9 jit_solution(18113353214381298801)
XLA Ops:
  0.6 1.4 %shard_map.146 = f32[1152,128]{1,0:T(8,128)S(1)} custom-call(bf16[1,128,512]{2,1,0:T(8,128)(2,1)} %query_ref.3, bf16[1,128,512]{2,1,0:T(8,128)(2,1)} %key_ref.3, bf16[1,128,512]{2,1,0:T(8,128)(2,1)} %value_ref.3, bf16[1,128,512]{2,1,0:T(8,128)(2,1)} %grad_ref.3, f32[128,512]{1,0:T(8,128)} %taps_ref.1), custom_call_target="tpu_custom_call" | custom-call | tf_op jit(solution)/shard_map/pallas_call | solution.py:248
  2.0 0.0 copy-start
  2.0 0.0 copy-start.1
  2.1 0.0 copy-start.6
  2.1 0.0 copy-start.7
  2.1 0.0 copy-start.8
  2.1 0.0 copy-start.9
  2.1 55.2 %all_to_all.20 = f32[128,9,1,128]{3,2,1,0:T(1,128)S(1)} all-to-all(f32[128,9,1,128]{3,2,1,0:T(1,128)S(1)} %bitcast.13), channel_id=1, replica_groups=mesh['y'=4,'zl'=4,'ctx'=32] {'zl','ctx'}, dimensions={0} | all-to-all | bytes 1179648 | tf_op jit(solution)/shard_map/all_to_all | solution.py:229
  57.4 0.0 copy-done
  57.4 0.0 copy-done.1
  57.4 0.0 copy-done.6
  57.4 0.0 copy-done.7
  57.4 0.0 copy-done.8
  57.4 0.0 copy-done.9
  57.4 2.0 %shard_map.147 = (f32[640,256]{1,0:T(8,128)S(1)}, f32[640,256]{1,0:T(8,128)S(1)}, f32[128,128]{1,0:T(8,128)}) custom-call(f32[1152,128]{1,0:T(8,128)S(1)} %bitcast.8, bf16[80,96]{1,0:T(8,128)(2,1)S(1)} %copy-done.6, f32[40,128]{1,0:T(8,128)S(1)} %copy-done.7, f32[40,128]{1,0:T(8,128)S(1)} %copy-done.8, bf16[768,256]{1,0:T(8,128)(2,1)S(1)} %copy-done, ...), custom_call_target="tpu_custom_call" | custom-call | tf_op jit(solution)/shard_map/pallas_call | solution.py:252
  59.4 4.5 %all-to-all-start.1 = ((f32[4,32,128]{2,1,0:T(8,128)}), f32[4,32,128]{2,1,0:T(8,128)S(1)}, u32[]{:S(2)}, u32[]{:S(2)}) async-start(f32[4,32,128]{2,1,0:T(8,128)} %bitcast.2), calls=%async_computation.1 | async-start | bytes 131072 | tf_op jit(solution)/shard_map/all_to_all | solution.py:234
  63.9 1.9 %shard_map.148.timed_ref = f32[1024,128]{1,0:T(8,128)S(1)} custom-call(f32[1152,128]{1,0:T(8,128)S(1)} %bitcast.9, f32[640,256]{1,0:T(8,128)S(1)} %get-tuple-element.13.gated_ref, f32[640,256]{1,0:T(8,128)S(1)} %get-tuple-element.14.grad_ref, bf16[80,96]{1,0:T(8,128)(2,1)S(1)} %copy-done.6, f32[40,128]{1,0:T(8,128)S(1)} %copy-done.7, ...), custom_call_target="tpu_custom_call" | custom-call | tf_op jit(solution)/shard_map/pallas_call | solution.py:256
  65.8 3.7 %all-to-all-done.1 = f32[4,32,128]{2,1,0:T(8,128)S(1)} async-done(((f32[4,32,128]{2,1,0:T(8,128)}), f32[4,32,128]{2,1,0:T(8,128)S(1)}, u32[]{:S(2)}, u32[]{:S(2)}) %all-to-all-start.1) | async-done | bytes 65568 | tf_op jit(solution)/shard_map/all_to_all | solution.py:234
  69.5 0.1 shard_map.149
  69.6 42.6 %all_to_all.21 = f32[128,9,1,128]{3,2,1,0:T(1,128)S(1)} all-to-all(f32[128,9,1,128]{3,2,1,0:T(1,128)S(1)} %bitcast.12), channel_id=1, replica_groups=mesh['y'=4,'zl'=4,'ctx'=32] {'zl','ctx'}, dimensions={0} | all-to-all | bytes 1179648 | tf_op jit(solution)/shard_map/all_to_all | solution.py:229
  112.2 0.8 shard_map.151
  113.0 0.0 copy-start.2
  113.0 0.0 copy-start.3
  113.0 0.0 copy-start.4
  113.0 3.6 %all-to-all-start.3 = ((f32[4,128,128]{2,1,0:T(8,128)}), f32[4,128,128]{2,1,0:T(8,128)S(1)}, u32[]{:S(2)}, u32[]{:S(2)}) async-start(f32[4,128,128]{2,1,0:T(8,128)} %bitcast.6), calls=%async_computation.3 | async-start | bytes 524288 | tf_op jit(solution)/shard_map/all_to_all | solution.py:234
  116.6 0.0 copy-done.2
  116.6 0.0 copy-done.3
  116.6 0.0 copy-done.4
  116.6 0.0 copy-done.5
  116.6 1.0 shard_map.150
  117.6 5.6 %all-to-all-done.3 = f32[4,128,128]{2,1,0:T(8,128)S(1)} async-done(((f32[4,128,128]{2,1,0:T(8,128)}), f32[4,128,128]{2,1,0:T(8,128)S(1)}, u32[]{:S(2)}, u32[]{:S(2)}) %all-to-all-start.3) | async-done | bytes 262176 | tf_op jit(solution)/shard_map/all_to_all | solution.py:234
  123.2 0.7 shard_map.152
  (1 shorter events, 0.0 us)
Async XLA Ops:
  2.0 55.3 %copy-start = (bf16[768,256]{1,0:T(8,128)(2,1)S(1)}, bf16[768,256]{1,0:T(8,128)(2,1)}, u32[]{:S(2)}) copy-start(bf16[768,256]{1,0:T(8,128)(2,1)} %constant.16.clone.full_ref) | copy-start | bytes 1179652
  2.0 55.3 %copy-start.1 = (bf16[768,256]{1,0:T(8,128)(2,1)S(1)}, bf16[768,256]{1,0:T(8,128)(2,1)}, u32[]{:S(2)}) copy-start(bf16[768,256]{1,0:T(8,128)(2,1)} %constant.17.clone.inv_full_ref) | copy-start | bytes 1179652
  2.1 55.3 %copy-start.6 = (bf16[80,96]{1,0:T(8,128)(2,1)S(1)}, bf16[80,96]{1,0:T(8,128)(2,1)}, u32[]{:S(2)}) copy-start(bf16[80,96]{1,0:T(8,128)(2,1)} %constant.12.clone.mix_ref) | copy-start | bytes 46084
  2.1 55.3 %copy-start.7 = (f32[40,128]{1,0:T(8,128)S(1)}, f32[40,128]{1,0:T(8,128)}, u32[]{:S(2)}) copy-start(f32[40,128]{1,0:T(8,128)} %constant.14.clone.cos_ref) | copy-start | bytes 61444
  2.1 55.3 %copy-start.8 = (f32[40,128]{1,0:T(8,128)S(1)}, f32[40,128]{1,0:T(8,128)}, u32[]{:S(2)}) copy-start(f32[40,128]{1,0:T(8,128)} %constant.15.clone.sin_ref) | copy-start | bytes 61444
  2.1 55.3 %copy-start.9 = (bf16[32,240]{1,0:T(8,128)(2,1)S(1)}, bf16[32,240]{1,0:T(8,128)(2,1)}, u32[]{:S(2)}) copy-start(bf16[32,240]{1,0:T(8,128)(2,1)} %constant.13.clone.inv_mix_ref) | copy-start | bytes 46084
  59.4 10.1 %all-to-all-start.1 = ((f32[4,32,128]{2,1,0:T(8,128)}), f32[4,32,128]{2,1,0:T(8,128)S(1)}, u32[]{:S(2)}, u32[]{:S(2)}) async-start(f32[4,32,128]{2,1,0:T(8,128)} %bitcast.2), calls=%async_computation.1 | async-start | bytes 131072 | tf_op jit(solution)/shard_map/all_to_all | solution.py:234
  113.0 3.6 %copy-start.2 = (bf16[1,128,512]{2,1,0:T(8,128)(2,1)S(1)}, bf16[1,128,512]{2,1,0:T(8,128)(2,1)}, u32[]{:S(2)}) copy-start(bf16[1,128,512]{2,1,0:T(8,128)(2,1)} %query_ref.3) | copy-start | bytes 393220
  113.0 3.6 %copy-start.3 = (bf16[1,128,512]{2,1,0:T(8,128)(2,1)S(1)}, bf16[1,128,512]{2,1,0:T(8,128)(2,1)}, u32[]{:S(2)}) copy-start(bf16[1,128,512]{2,1,0:T(8,128)(2,1)} %key_ref.3) | copy-start | bytes 393220
  113.0 3.6 %copy-start.4 = (bf16[1,128,512]{2,1,0:T(8,128)(2,1)S(1)}, bf16[1,128,512]{2,1,0:T(8,128)(2,1)}, u32[]{:S(2)}) copy-start(bf16[1,128,512]{2,1,0:T(8,128)(2,1)} %value_ref.3) | copy-start | bytes 393220
  113.0 3.6 %copy-start.5 = (bf16[1,128,512]{2,1,0:T(8,128)(2,1)S(1)}, bf16[1,128,512]{2,1,0:T(8,128)(2,1)}, u32[]{:S(2)}) copy-start(bf16[1,128,512]{2,1,0:T(8,128)(2,1)} %grad_ref.3) | copy-start | bytes 393220
  113.0 10.2 %all-to-all-start.3 = ((f32[4,128,128]{2,1,0:T(8,128)}), f32[4,128,128]{2,1,0:T(8,128)S(1)}, u32[]{:S(2)}, u32[]{:S(2)}) async-start(f32[4,128,128]{2,1,0:T(8,128)} %bitcast.6), calls=%async_computation.3 | async-start | bytes 524288 | tf_op jit(solution)/shard_map/all_to_all | solution.py:234

commit v4 on v2

--- a/solution.py
+++ b/solution.py
@@ -19,6 +19,7 @@
 PERIOD = 2 * NB * BLK
 VMEM = pl.BlockSpec(memory_space=pltpu.VMEM)
 HBM = pl.BlockSpec(memory_space=pltpu.HBM)
+SMALL = pltpu.CompilerParams(vmem_limit_bytes=8 * 1024 * 1024)
 PARAMS = pltpu.CompilerParams(vmem_limit_bytes=40 * 1024 * 1024)
 
 
@@ -235,8 +236,8 @@
         pltpu.VMEM((BLK, BLK), jnp.float32),
         pltpu.SemaphoreType.DMA((5,)),
     ]
-    sent = call(send_kernel, f32(peers * IN_ROWS, BLK), 5, HBM, None, scratch_shapes=scratch)(
-        queries, keys, values, grad_out, filter_taps
+    sent = call(send_kernel, f32(peers * IN_ROWS, BLK), 5, HBM, SMALL, scratch_shapes=scratch)(
+        *(pltpu.with_memory_space_constraint(a, pltpu.HBM) for a in (queries, keys, values, grad_out, filter_taps))
     )
     rows = exchange(sent, IN_ROWS)
     gated, grad, lag = call(forward_kernel, (f32(wide, 2 * BLK), f32(wide, 2 * BLK), f32(4 * peers, BLK)), 7)(

time: 124 us -> 123 us (level)
  no operation moved by 1% of the time
where the time goes in v4:
time: 123 us
  blocking collectives  106 us (86%)
  Pallas kernels  6.66 us (5%)
  waiting for transfers between devices  4.75 us (4%)
  starting transfers between devices  4.46 us (4%)
    all_to_all x2, blocking collectives, exchange(): lax.all_to_all(rows.reshape(peers, per, 1, BLK), ('zl', 'ctx'), 0, 0, til...  106 us
    all_to_all x1, waiting for transfers between devices, local(): lax.all_to_all(lag.reshape(4, peers, BLK), 'y', 0, 0, tiled=True)  4.75 us
    all_to_all x1, starting transfers between devices, local(): lax.all_to_all(lag.reshape(4, peers, BLK), 'y', 0, 0, tiled=True)  4.46 us
  transfers between devices with their start and end apart: 1, of which 1 were waited for; matrix products, arithmetic and copies ran while one was open for 0% of the time, Pallas kernels for 2%

profile of v4, /device:TPU:32, one launch (start us, length us, event | category | flops | bytes accessed | tf_op | source)
XLA Modules:
  0.0 122.9 jit_solution(4608552419257606554)
XLA Ops:
  0.6 1.4 %shard_map.146 = f32[1152,128]{1,0:T(8,128)S(1)} custom-call(bf16[1,128,512]{2,1,0:T(8,128)(2,1)} %refs_1_.1, bf16[1,128,512]{2,1,0:T(8,128)(2,1)} %refs_2_.1, bf16[1,128,512]{2,1,0:T(8,128)(2,1)} %refs_3_.1, bf16[1,128,512]{2,1,0:T(8,128)(2,1)} %refs_4_.1, f32[128,512]{1,0:T(8,128)} %taps_ref.1), custom_call_target="tpu_custom_call" | custom-call | tf_op jit(solution)/shard_map/pallas_call | solution.py:239
  2.0 0.0 copy-start
  2.0 0.0 copy-start.1
  2.1 0.0 copy-start.6
  2.1 0.0 copy-start.7
  2.1 0.0 copy-start.8
  2.1 0.0 copy-start.9
  2.1 55.2 %all_to_all.15 = f32[128,9,1,128]{3,2,1,0:T(1,128)S(1)} all-to-all(f32[128,9,1,128]{3,2,1,0:T(1,128)S(1)} %bitcast.10), channel_id=1, replica_groups=mesh['y'=4,'zl'=4,'ctx'=32] {'zl','ctx'}, dimensions={0} | all-to-all | bytes 1179648 | tf_op jit(solution)/shard_map/all_to_all | solution.py:225
  57.4 0.0 copy-done
  57.4 0.0 copy-done.1
  57.4 0.0 copy-done.6
  57.4 0.0 copy-done.7
  57.4 0.0 copy-done.8
  57.4 0.0 copy-done.9
  57.4 2.1 %shard_map.147 = (f32[640,256]{1,0:T(8,128)S(1)}, f32[640,256]{1,0:T(8,128)S(1)}, f32[512,128]{1,0:T(8,128)}) custom-call(f32[1152,128]{1,0:T(8,128)S(1)} %bitcast.6, bf16[80,96]{1,0:T(8,128)(2,1)S(1)} %copy-done.6, f32[40,128]{1,0:T(8,128)S(1)} %copy-done.7, f32[40,128]{1,0:T(8,128)S(1)} %copy-done.8, bf16[768,256]{1,0:T(8,128)(2,1)S(1)} %copy-done, ...), custom_call_target="tpu_custom_call" | custom-call | tf_op jit(solution)/shard_map/pallas_call | solution.py:243
  59.5 4.5 %all-to-all-start.1 = ((f32[4,128,128]{2,1,0:T(8,128)}), f32[4,128,128]{2,1,0:T(8,128)S(1)}, u32[]{:S(2)}, u32[]{:S(2)}) async-start(f32[4,128,128]{2,1,0:T(8,128)} %bitcast.2), calls=%async_computation.1 | async-start | bytes 524288 | tf_op jit(solution)/shard_map/all_to_all | solution.py:246
  64.0 1.9 %shard_map.148.timed_ref = f32[1024,128]{1,0:T(8,128)S(1)} custom-call(f32[1152,128]{1,0:T(8,128)S(1)} %bitcast.7, f32[640,256]{1,0:T(8,128)S(1)} %get-tuple-element.9.gated_ref, f32[640,256]{1,0:T(8,128)S(1)} %get-tuple-element.10.grad_ref, bf16[80,96]{1,0:T(8,128)(2,1)S(1)} %copy-done.6, f32[40,128]{1,0:T(8,128)S(1)} %copy-done.7, ...), custom_call_target="tpu_custom_call" | custom-call | tf_op jit(solution)/shard_map/pallas_call | solution.py:247
  65.9 4.7 %all-to-all-done.1 = f32[4,128,128]{2,1,0:T(8,128)S(1)} async-done(((f32[4,128,128]{2,1,0:T(8,128)}), f32[4,128,128]{2,1,0:T(8,128)S(1)}, u32[]{:S(2)}, u32[]{:S(2)}) %all-to-all-start.1) | async-done | bytes 262176 | tf_op jit(solution)/shard_map/all_to_all | solution.py:246
  70.6 0.1 shard_map.149
  70.8 0.0 copy-start.2
  70.8 0.0 copy-start.3
  70.8 0.0 copy-start.4
  70.8 0.0 copy-start.5
  70.8 50.9 %all_to_all.16 = f32[128,12,1,128]{3,2,1,0:T(1,128)S(1)} all-to-all(f32[128,12,1,128]{3,2,1,0:T(1,128)S(1)} %bitcast.9), channel_id=1, replica_groups=mesh['y'=4,'zl'=4,'ctx'=32] {'zl','ctx'}, dimensions={0} | all-to-all | bytes 1572864 | tf_op jit(solution)/shard_map/all_to_all | solution.py:225
  121.7 0.0 copy-done.2
  121.7 0.0 copy-done.3
  121.7 0.0 copy-done.4
  121.8 0.0 copy-done.5
  121.8 1.1 shard_map.150
Async XLA Ops:
  2.0 55.3 %copy-start = (bf16[768,256]{1,0:T(8,128)(2,1)S(1)}, bf16[768,256]{1,0:T(8,128)(2,1)}, u32[]{:S(2)}) copy-start(bf16[768,256]{1,0:T(8,128)(2,1)} %constant.16.clone.full_ref) | copy-start | bytes 1179652
  2.0 55.3 %copy-start.1 = (bf16[768,256]{1,0:T(8,128)(2,1)S(1)}, bf16[768,256]{1,0:T(8,128)(2,1)}, u32[]{:S(2)}) copy-start(bf16[768,256]{1,0:T(8,128)(2,1)} %constant.17.clone.inv_full_ref) | copy-start | bytes 1179652
  2.1 55.3 %copy-start.6 = (bf16[80,96]{1,0:T(8,128)(2,1)S(1)}, bf16[80,96]{1,0:T(8,128)(2,1)}, u32[]{:S(2)}) copy-start(bf16[80,96]{1,0:T(8,128)(2,1)} %constant.12.clone.mix_ref) | copy-start | bytes 46084
  2.1 55.3 %copy-start.7 = (f32[40,128]{1,0:T(8,128)S(1)}, f32[40,128]{1,0:T(8,128)}, u32[]{:S(2)}) copy-start(f32[40,128]{1,0:T(8,128)} %constant.14.clone.cos_ref) | copy-start | bytes 61444
  2.1 55.3 %copy-start.8 = (f32[40,128]{1,0:T(8,128)S(1)}, f32[40,128]{1,0:T(8,128)}, u32[]{:S(2)}) copy-start(f32[40,128]{1,0:T(8,128)} %constant.15.clone.sin_ref) | copy-start | bytes 61444
  2.1 55.3 %copy-start.9 = (bf16[32,240]{1,0:T(8,128)(2,1)S(1)}, bf16[32,240]{1,0:T(8,128)(2,1)}, u32[]{:S(2)}) copy-start(bf16[32,240]{1,0:T(8,128)(2,1)} %constant.13.clone.inv_mix_ref) | copy-start | bytes 46084
  59.5 11.1 %all-to-all-start.1 = ((f32[4,128,128]{2,1,0:T(8,128)}), f32[4,128,128]{2,1,0:T(8,128)S(1)}, u32[]{:S(2)}, u32[]{:S(2)}) async-start(f32[4,128,128]{2,1,0:T(8,128)} %bitcast.2), calls=%async_computation.1 | async-start | bytes 524288 | tf_op jit(solution)/shard_map/all_to_all | solution.py:246
  70.8 51.0 %copy-start.2 = (bf16[1,128,512]{2,1,0:T(8,128)(2,1)S(1)}, bf16[1,128,512]{2,1,0:T(8,128)(2,1)}, u32[]{:S(2)}) copy-start(bf16[1,128,512]{2,1,0:T(8,128)(2,1)} %refs_1_.1) | copy-start | bytes 393220
  70.8 51.0 %copy-start.3 = (bf16[1,128,512]{2,1,0:T(8,128)(2,1)S(1)}, bf16[1,128,512]{2,1,0:T(8,128)(2,1)}, u32[]{:S(2)}) copy-start(bf16[1,128,512]{2,1,0:T(8,128)(2,1)} %refs_2_.1) | copy-start | bytes 393220
  70.8 51.0 %copy-start.4 = (bf16[1,128,512]{2,1,0:T(8,128)(2,1)S(1)}, bf16[1,128,512]{2,1,0:T(8,128)(2,1)}, u32[]{:S(2)}) copy-start(bf16[1,128,512]{2,1,0:T(8,128)(2,1)} %refs_3_.1) | copy-start | bytes 393220
  70.8 51.0 %copy-start.5 = (bf16[1,128,512]{2,1,0:T(8,128)(2,1)S(1)}, bf16[1,128,512]{2,1,0:T(8,128)(2,1)}, u32[]{:S(2)}) copy-start(bf16[1,128,512]{2,1,0:T(8,128)(2,1)} %refs_4_.1) | copy-start | bytes 393220

commit v5 on v4

--- a/solution.py
+++ b/solution.py
@@ -13,10 +13,11 @@
 BLK = 128
 NB = 32
 CG = 4
-KH = 40
+TILE = 8
 IN_ROWS = 2 * CG + 1
 OUT_ROWS = 3 * CG
 PERIOD = 2 * NB * BLK
+SPAN = 2 * CG * NB + TILE
 VMEM = pl.BlockSpec(memory_space=pltpu.VMEM)
 HBM = pl.BlockSpec(memory_space=pltpu.HBM)
 SMALL = pltpu.CompilerParams(vmem_limit_bytes=8 * 1024 * 1024)
@@ -30,21 +31,21 @@
 
 
 def tables():
-    k1 = np.arange(KH)
-    used = (k1 <= NB)[:, None]
+    k1 = np.arange(NB)
     block = np.arange(NB)
     angle = 2.0 * np.pi * ((k1[:, None] * block[None, :]) % (2 * NB)) / (2 * NB)
-    mix = np.concatenate([np.cos(angle) * used, -np.sin(angle) * used], 0)
-    high, low = high_low(mix)
+    last = np.tile(1.0 - 2.0 * (block % 2), (TILE, 1))
+    high, low = high_low(np.concatenate([np.cos(angle), -np.sin(angle), last], 0))
     forward_mix = np.concatenate([high, high, low], 1)
-    weight = np.where((k1 == 0) | (k1 == NB), 1.0, 2.0)[:, None] * used / PERIOD
-    back = np.concatenate([np.cos(angle) * weight, -np.sin(angle) * weight], 0).T
+    weight = np.where(k1 == 0, 1.0, 2.0)[:, None] / PERIOD
+    back = np.concatenate([np.cos(angle) * weight, -np.sin(angle) * weight, last / PERIOD, 0.0 * last], 0).T
     high, low = high_low(back)
     inverse_mix = np.concatenate([high, high, low], 1)
     offset = np.arange(BLK)
-    turn = 2.0 * np.pi * (k1[:, None] * offset[None, :]) / PERIOD
-    cos_turn = (np.cos(turn) * used).astype(np.float32)
-    sin_turn = (np.sin(turn) * used).astype(np.float32)
+    harmonic = np.concatenate([k1, np.full(TILE, NB)])
+    turn = 2.0 * np.pi * (harmonic[:, None] * offset[None, :]) / PERIOD
+    cos_turn = np.cos(turn).astype(np.float32)
+    sin_turn = np.sin(turn).astype(np.float32)
     full = 2.0 * np.pi * ((offset[:, None] * offset[None, :]) % BLK) / BLK
     cos, sin = np.cos(full), np.sin(full)
     high, low = high_low(np.block([[cos, -sin], [sin, cos]]))
@@ -74,29 +75,38 @@
     return dot(jnp.concatenate([high, low, high], 1), table_ref[...])
 
 
+def tile_row():
+    return lax.broadcasted_iota(jnp.int32, (TILE, BLK), 0)
+
+
 def spectra(blocks, mix, cos_turn, sin_turn, full_ref):
     mixed = mix_rows(mix, jnp.concatenate(blocks, 1))
+    cos, sin = cos_turn[:NB], sin_turn[:NB]
     turned = []
+    last = jnp.zeros((TILE, BLK), jnp.float32)
+    own = tile_row() % len(blocks)
     for index in range(len(blocks)):
         lanes = slice(index * BLK, (index + 1) * BLK)
-        real, imag = mixed[:KH, lanes], mixed[KH:, lanes]
-        turned.append(
-            jnp.concatenate(
-                [real * cos_turn + imag * sin_turn, imag * cos_turn - real * sin_turn], 1
-            )
-        )
+        real, imag = mixed[:NB, lanes], mixed[NB : 2 * NB, lanes]
+        turned.append(jnp.concatenate([real * cos + imag * sin, imag * cos - real * sin], 1))
+        last = jnp.where(own == index, mixed[2 * NB :, lanes], last)
+    turned.append(jnp.concatenate([last * cos_turn[NB:], -last * sin_turn[NB:]], 1))
     return full_transform(jnp.concatenate(turned, 0), full_ref)
 
 
 def positions(spectrum, count, mix, cos_turn, sin_turn, full_ref):
     back = full_transform(spectrum, full_ref)
+    cos, sin = cos_turn[:NB], sin_turn[:NB]
+    last = back[count * NB :, :BLK] * cos_turn[NB:] - back[count * NB :, BLK:] * sin_turn[NB:]
+    own = tile_row()
+    empty = jnp.zeros((TILE, BLK), jnp.float32)
     columns = []
     for index in range(count):
-        rows = slice(index * KH, (index + 1) * KH)
+        rows = slice(index * NB, (index + 1) * NB)
         real, imag = back[rows, :BLK], back[rows, BLK:]
         columns.append(
             jnp.concatenate(
-                [real * cos_turn - imag * sin_turn, imag * cos_turn + real * sin_turn], 0
+                [real * cos - imag * sin, imag * cos + real * sin, jnp.where(own == index, last, empty), empty], 0
             )
         )
     return mix_rows(mix, jnp.concatenate(columns, 1))
@@ -129,20 +139,19 @@
     return rows_ref[pl.ds(seq * NB * IN_ROWS + row, NB, IN_ROWS), :]
 
 
-def forward_kernel(
-    rows_ref, mix_ref, cos_ref, sin_ref, full_ref, inv_mix_ref, inv_full_ref, gated_ref, grad_ref, lag_ref
-):
+def forward_kernel(rows_ref, mix_ref, cos_ref, sin_ref, full_ref, inv_mix_ref, inv_full_ref, both_ref, lag_ref):
     mix, cos_turn, sin_turn = mix_ref[...], cos_ref[...], sin_ref[...]
-    wide = CG * KH
+    wide = CG * NB
     lag = None
     for seq in range(CG):
         blocks = [block(rows_ref, seq, row) for row in range(2 * CG)]
         both = spectra(blocks, mix, cos_turn, sin_turn, full_ref)
-        rows = slice(seq * wide, (seq + 1) * wide)
-        gated_ref[rows, :] = both[:wide]
-        grad_ref[rows, :] = both[wide:]
-        gated_re, gated_im = both[:wide, :BLK], both[:wide, BLK:]
-        grad_re, grad_im = both[wide:, :BLK], both[wide:, BLK:]
+        both_ref[seq * SPAN : (seq + 1) * SPAN, :] = both
+        last = both[2 * wide :]
+        gated = jnp.concatenate([both[:wide], last], 0)
+        grad = jnp.concatenate([both[wide : 2 * wide], last[CG:], last[:CG]], 0)
+        gated_re, gated_im = gated[:, :BLK], gated[:, BLK:]
+        grad_re, grad_im = grad[:, :BLK], grad[:, BLK:]
         term = jnp.concatenate(
             [grad_re * gated_re + grad_im * gated_im, grad_im * gated_re - grad_re * gated_im], 1
         )
@@ -155,24 +164,20 @@
 
 
 def inverse_kernel(
-    rows_ref, gated_ref, grad_ref, mix_ref, cos_ref, sin_ref, full_ref, inv_mix_ref, inv_full_ref, out_ref
+    rows_ref, both_ref, mix_ref, cos_ref, sin_ref, full_ref, inv_mix_ref, inv_full_ref, out_ref
 ):
     mix, cos_turn, sin_turn = mix_ref[...], cos_ref[...], sin_ref[...]
     inv_mix = inv_mix_ref[...]
-    wide = CG * KH
+    wide = CG * NB
     taps = spectra([block(rows_ref, part, 2 * CG) for part in range(CG)], mix, cos_turn, sin_turn, full_ref)
-    taps_re, taps_im = taps[:, :BLK], taps[:, BLK:]
+    low_im, last_im = taps[:wide, BLK:], taps[wide:, BLK:]
+    taps_re = jnp.concatenate([taps[:wide, :BLK], taps[:wide, :BLK], taps[wide:, :BLK]], 0)
+    taps_im = jnp.concatenate([low_im, -low_im, jnp.where(tile_row() < CG, last_im, -last_im)], 0)
     for seq in range(CG):
-        rows = slice(seq * wide, (seq + 1) * wide)
-        gated_re, gated_im = gated_ref[rows, :BLK], gated_ref[rows, BLK:]
-        grad_re, grad_im = grad_ref[rows, :BLK], grad_ref[rows, BLK:]
-        conv = jnp.concatenate(
-            [taps_re * gated_re - taps_im * gated_im, taps_re * gated_im + taps_im * gated_re], 1
-        )
-        back = jnp.concatenate(
-            [taps_re * grad_re + taps_im * grad_im, taps_re * grad_im - taps_im * grad_re], 1
-        )
-        timed = positions(jnp.concatenate([conv, back], 0), 2 * CG, inv_mix, cos_turn, sin_turn, inv_full_ref)
+        rows = slice(seq * SPAN, (seq + 1) * SPAN)
+        real, imag = both_ref[rows, :BLK], both_ref[rows, BLK:]
+        product = jnp.concatenate([taps_re * real - taps_im * imag, taps_re * imag + taps_im * real], 1)
+        timed = positions(product, 2 * CG, inv_mix, cos_turn, sin_turn, inv_full_ref)
         for row in range(2 * CG):
             out_ref[pl.ds(seq * NB * 2 * CG + row, NB, 2 * CG), :] = timed[:, row * BLK : (row + 1) * BLK]
 
@@ -189,28 +194,42 @@
             out_ref[pl.ds(first, NB, OUT_ROWS), :] = lag[part * NB : (part + 1) * NB, :]
 
 
-def finish_kernel(
-    scale, rows_ref, query_ref, key_ref, value_ref, grad_ref, conv_out_ref, gq_ref, gk_ref, gv_ref, gf_ref
-):
-    for part in range(CG):
-        lanes = slice(part * BLK, (part + 1) * BLK)
-        conv_s = rows_ref[pl.ds(part, BLK, OUT_ROWS), :].T
-        grad_z = rows_ref[pl.ds(CG + part, BLK, OUT_ROWS), :].T
-        lag = rows_ref[pl.ds(2 * CG + part, BLK, OUT_ROWS), :].T
-        conv_out_ref[0, :, lanes] = (query_ref[0, :, lanes].astype(jnp.float32) * conv_s).astype(jnp.bfloat16)
-        gq_ref[0, :, lanes] = (grad_ref[0, :, lanes].astype(jnp.float32) * conv_s).astype(jnp.bfloat16)
-        gk_ref[0, :, lanes] = (grad_z * value_ref[0, :, lanes].astype(jnp.float32)).astype(jnp.bfloat16)
-        gv_ref[0, :, lanes] = (grad_z * key_ref[0, :, lanes].astype(jnp.float32)).astype(jnp.bfloat16)
-        gf_ref[:, lanes] = lag * scale
-
-
-def call(kernel, out_shape, count, space=VMEM, params=PARAMS, **kwargs):
+def finish_kernel(scale, rows_ref, query_ref, key_ref, value_ref, grad_ref, *refs):
+    results, (conv_out, gq, gk, gv, gf, sems) = refs[:5], refs[5:]
+    held = (conv_out, gq, gk, gv, gf)
+    copies = [pltpu.make_async_copy(held[index], results[index], sems.at[index]) for index in range(5)]
+
+    def column(row):
+        return rows_ref[pl.ds(row, BLK, OUT_ROWS), :].T
+
+    for part in range(CG):
+        gf[:, part * BLK : (part + 1) * BLK] = column(2 * CG + part) * scale
+    copies[4].start()
+    for part in range(CG):
+        lanes = slice(part * BLK, (part + 1) * BLK)
+        conv_s = column(part)
+        conv_out[0, :, lanes] = (query_ref[0, :, lanes].astype(jnp.float32) * conv_s).astype(jnp.bfloat16)
+        gq[0, :, lanes] = (grad_ref[0, :, lanes].astype(jnp.float32) * conv_s).astype(jnp.bfloat16)
+    copies[0].start()
+    copies[1].start()
+    for part in range(CG):
+        lanes = slice(part * BLK, (part + 1) * BLK)
+        grad_z = column(CG + part)
+        gk[0, :, lanes] = (grad_z * value_ref[0, :, lanes].astype(jnp.float32)).astype(jnp.bfloat16)
+        gv[0, :, lanes] = (grad_z * key_ref[0, :, lanes].astype(jnp.float32)).astype(jnp.bfloat16)
+    copies[2].start()
+    copies[3].start()
+    for copy in copies:
+        copy.wait()
+
+
+def call(kernel, out_shape, count, space=VMEM, params=PARAMS, out_space=VMEM, **kwargs):
     single = not isinstance(out_shape, (tuple, list))
     return pl.pallas_call(
         kernel,
         out_shape=out_shape,
         in_specs=[space] * count,
-        out_specs=VMEM if single else [VMEM] * len(out_shape),
+        out_specs=out_space if single else [out_space] * len(out_shape),
         compiler_params=params,
         **kwargs,
     )
@@ -231,7 +250,6 @@
         jnp.asarray(t) for t in tables()
     )
     peers = CG * NB
-    wide = CG * CG * KH
     scratch = [pltpu.VMEM(queries.shape, jnp.bfloat16)] * 4 + [
         pltpu.VMEM((BLK, BLK), jnp.float32),
         pltpu.SemaphoreType.DMA((5,)),
@@ -240,25 +258,32 @@
         *(pltpu.with_memory_space_constraint(a, pltpu.HBM) for a in (queries, keys, values, grad_out, filter_taps))
     )
     rows = exchange(sent, IN_ROWS)
-    gated, grad, lag = call(forward_kernel, (f32(wide, 2 * BLK), f32(wide, 2 * BLK), f32(4 * peers, BLK)), 7)(
+    both, lag = call(forward_kernel, (f32(CG * SPAN, 2 * BLK), f32(4 * peers, BLK)), 7)(
         rows, forward_mix, cos_turn, sin_turn, forward_full, inverse_mix, inverse_full
     )
     shares = lax.all_to_all(lag.reshape(4, peers, BLK), "y", 0, 0, tiled=True).reshape(4 * peers, BLK)
-    timed = call(inverse_kernel, f32(peers * 2 * CG, BLK), 9)(
-        rows, gated, grad, forward_mix, cos_turn, sin_turn, forward_full, inverse_mix, inverse_full
+    timed = call(inverse_kernel, f32(peers * 2 * CG, BLK), 8)(
+        rows, both, forward_mix, cos_turn, sin_turn, forward_full, inverse_mix, inverse_full
     )
     joined = call(join_kernel, f32(peers * OUT_ROWS, BLK), 2)(shares, timed)
     returned = exchange(joined, OUT_ROWS)
     scale = 1.0 / math.sqrt(16 * NB * BLK)
     shape = jax.ShapeDtypeStruct(queries.shape, jnp.bfloat16)
 
+    taps_shape = f32(*filter_taps.shape)
+    held = [pltpu.VMEM(shape.shape, jnp.bfloat16)] * 4 + [pltpu.VMEM(taps_shape.shape, jnp.float32)]
+
     def finish(*refs):
         finish_kernel(scale, *refs)
 
     return tuple(
-        call(finish, (shape, shape, shape, shape, f32(*filter_taps.shape)), 5)(
-            returned, queries, keys, values, grad_out
-        )
+        call(
+            finish,
+            (shape, shape, shape, shape, taps_shape),
+            5,
+            out_space=HBM,
+            scratch_shapes=[*held, pltpu.SemaphoreType.DMA((5,))],
+        )(returned, queries, keys, values, grad_out)
     )
 
 

time: 123 us -> 123 us (level)
  no operation moved by 1% of the time
where the time goes in v5:
time: 123 us
  blocking collectives  106 us (86%)
  Pallas kernels  6.71 us (5%)
  waiting for transfers between devices  4.61 us (4%)
  starting transfers between devices  4.46 us (4%)
    all_to_all x2, blocking collectives, exchange(): lax.all_to_all(rows.reshape(peers, per, 1, BLK), ('zl', 'ctx'), 0, 0, til...  106 us
    all_to_all x1, waiting for transfers between devices, local(): lax.all_to_all(lag.reshape(4, peers, BLK), 'y', 0, 0, tiled=True)  4.61 us
    all_to_all x1, starting transfers between devices, local(): lax.all_to_all(lag.reshape(4, peers, BLK), 'y', 0, 0, tiled=True)  4.46 us
  transfers between devices with their start and end apart: 1, of which 1 were waited for; matrix products, arithmetic and copies ran while one was open for 0% of the time, Pallas kernels for 2%

profile of v5, /device:TPU:32, one launch (start us, length us, event | category | flops | bytes accessed | tf_op | source)
XLA Modules:
  0.0 122.7 jit_solution(1603158754837708432)
XLA Ops:
  0.6 0.0 copy-start
  0.6 0.0 copy-start.1
  0.7 0.0 copy-start.6
  0.7 0.0 copy-start.7
  0.7 0.0 copy-start.8
  0.7 0.0 copy-start.9
  0.7 1.4 %shard_map.146 = f32[1152,128]{1,0:T(8,128)S(1)} custom-call(bf16[1,128,512]{2,1,0:T(8,128)(2,1)} %refs_1_.1, bf16[1,128,512]{2,1,0:T(8,128)(2,1)} %refs_2_.1, bf16[1,128,512]{2,1,0:T(8,128)(2,1)} %refs_3_.1, bf16[1,128,512]{2,1,0:T(8,128)(2,1)} %refs_4_.1, f32[128,512]{1,0:T(8,128)} %taps_ref.1), custom_call_target="tpu_custom_call" | custom-call | tf_op jit(solution)/shard_map/pallas_call | solution.py:257
  2.2 55.1 %all_to_all.15 = f32[128,9,1,128]{3,2,1,0:T(1,128)S(1)} all-to-all(f32[128,9,1,128]{3,2,1,0:T(1,128)S(1)} %bitcast.10), channel_id=1, replica_groups=mesh['y'=4,'zl'=4,'ctx'=32] {'zl','ctx'}, dimensions={0} | all-to-all | bytes 1179648 | tf_op jit(solution)/shard_map/all_to_all | solution.py:244
  57.3 0.0 copy-done
  57.3 0.0 copy-done.1
  57.3 0.0 copy-done.6
  57.3 0.0 copy-done.7
  57.3 0.0 copy-done.8
  57.3 0.0 copy-done.9
  57.3 2.0 %shard_map.147 = (f32[1056,256]{1,0:T(8,128)S(1)}, f32[512,128]{1,0:T(8,128)}) custom-call(f32[1152,128]{1,0:T(8,128)S(1)} %bitcast.6, bf16[72,96]{1,0:T(8,128)(2,1)S(1)} %copy-done.8, f32[40,128]{1,0:T(8,128)S(1)} %copy-done.6, f32[40,128]{1,0:T(8,128)S(1)} %copy-done.7, bf16[768,256]{1,0:T(8,128)(2,1)S(1)} %copy-done, bf16[32,240]{1,0:T(8,128)(2,1)S(1)} %copy-done.9, ...), custom_call_target="tpu_custom_call" | custom-call | tf_op jit(solution)/shard_map/pallas_call | solution.py:261
  59.3 4.5 %all-to-all-start.1 = ((f32[4,128,128]{2,1,0:T(8,128)}), f32[4,128,128]{2,1,0:T(8,128)S(1)}, u32[]{:S(2)}, u32[]{:S(2)}) async-start(f32[4,128,128]{2,1,0:T(8,128)} %bitcast.2), calls=%async_computation.1 | async-start | bytes 524288 | tf_op jit(solution)/shard_map/all_to_all | solution.py:264
  63.8 2.1 %shard_map.148.timed_ref = f32[1024,128]{1,0:T(8,128)S(1)} custom-call(f32[1152,128]{1,0:T(8,128)S(1)} %bitcast.7, f32[1056,256]{1,0:T(8,128)S(1)} %get-tuple-element.8.both_ref, bf16[72,96]{1,0:T(8,128)(2,1)S(1)} %copy-done.8, f32[40,128]{1,0:T(8,128)S(1)} %copy-done.6, f32[40,128]{1,0:T(8,128)S(1)} %copy-done.7, bf16[768,256]{1,0:T(8,128)(2,1)S(1)} %copy-done, ...), custom_call_target="tpu_custom_call" | custom-call | tf_op jit(solution)/shard_map/pallas_call | solution.py:265
  65.9 4.6 %all-to-all-done.1 = f32[4,128,128]{2,1,0:T(8,128)S(1)} async-done(((f32[4,128,128]{2,1,0:T(8,128)}), f32[4,128,128]{2,1,0:T(8,128)S(1)}, u32[]{:S(2)}, u32[]{:S(2)}) %all-to-all-start.1) | async-done | bytes 262176 | tf_op jit(solution)/shard_map/all_to_all | solution.py:264
  70.5 0.1 shard_map.149
  70.6 0.0 copy-start.2
  70.6 0.0 copy-start.3
  70.6 0.0 copy-start.4
  70.6 0.0 copy-start.5
  70.7 50.9 %all_to_all.16 = f32[128,12,1,128]{3,2,1,0:T(1,128)S(1)} all-to-all(f32[128,12,1,128]{3,2,1,0:T(1,128)S(1)} %bitcast.9), channel_id=1, replica_groups=mesh['y'=4,'zl'=4,'ctx'=32] {'zl','ctx'}, dimensions={0} | all-to-all | bytes 1572864 | tf_op jit(solution)/shard_map/all_to_all | solution.py:244
  121.6 0.0 copy-done.2
  121.6 0.0 copy-done.3
  121.6 0.0 copy-done.4
  121.6 0.0 copy-done.5
  121.6 1.1 shard_map.150
Async XLA Ops:
  0.6 56.6 %copy-start = (bf16[768,256]{1,0:T(8,128)(2,1)S(1)}, bf16[768,256]{1,0:T(8,128)(2,1)}, u32[]{:S(2)}) copy-start(bf16[768,256]{1,0:T(8,128)(2,1)} %constant.16.clone.full_ref) | copy-start | bytes 1179652
  0.6 56.6 %copy-start.1 = (bf16[768,256]{1,0:T(8,128)(2,1)S(1)}, bf16[768,256]{1,0:T(8,128)(2,1)}, u32[]{:S(2)}) copy-start(bf16[768,256]{1,0:T(8,128)(2,1)} %constant.17.clone.inv_full_ref) | copy-start | bytes 1179652
  0.7 56.6 %copy-start.6 = (f32[40,128]{1,0:T(8,128)S(1)}, f32[40,128]{1,0:T(8,128)}, u32[]{:S(2)}) copy-start(f32[40,128]{1,0:T(8,128)} %constant.14.clone.cos_ref) | copy-start | bytes 61444
  0.7 56.6 %copy-start.7 = (f32[40,128]{1,0:T(8,128)S(1)}, f32[40,128]{1,0:T(8,128)}, u32[]{:S(2)}) copy-start(f32[40,128]{1,0:T(8,128)} %constant.15.clone.sin_ref) | copy-start | bytes 61444
  0.7 56.6 %copy-start.8 = (bf16[72,96]{1,0:T(8,128)(2,1)S(1)}, bf16[72,96]{1,0:T(8,128)(2,1)}, u32[]{:S(2)}) copy-start(bf16[72,96]{1,0:T(8,128)(2,1)} %constant.12.clone.mix_ref) | copy-start | bytes 41476
  0.7 56.6 %copy-start.9 = (bf16[32,240]{1,0:T(8,128)(2,1)S(1)}, bf16[32,240]{1,0:T(8,128)(2,1)}, u32[]{:S(2)}) copy-start(bf16[32,240]{1,0:T(8,128)(2,1)} %constant.13.clone.inv_mix_ref) | copy-start | bytes 46084
  59.3 11.1 %all-to-all-start.1 = ((f32[4,128,128]{2,1,0:T(8,128)}), f32[4,128,128]{2,1,0:T(8,128)S(1)}, u32[]{:S(2)}, u32[]{:S(2)}) async-start(f32[4,128,128]{2,1,0:T(8,128)} %bitcast.2), calls=%async_computation.1 | async-start | bytes 524288 | tf_op jit(solution)/shard_map/all_to_all | solution.py:264
  70.6 51.0 %copy-start.2 = (bf16[1,128,512]{2,1,0:T(8,128)(2,1)S(1)}, bf16[1,128,512]{2,1,0:T(8,128)(2,1)}, u32[]{:S(2)}) copy-start(bf16[1,128,512]{2,1,0:T(8,128)(2,1)} %refs_1_.1) | copy-start | bytes 393220
  70.6 51.0 %copy-start.3 = (bf16[1,128,512]{2,1,0:T(8,128)(2,1)S(1)}, bf16[1,128,512]{2,1,0:T(8,128)(2,1)}, u32[]{:S(2)}) copy-start(bf16[1,128,512]{2,1,0:T(8,128)(2,1)} %refs_2_.1) | copy-start | bytes 393220
  70.6 51.0 %copy-start.4 = (bf16[1,128,512]{2,1,0:T(8,128)(2,1)S(1)}, bf16[1,128,512]{2,1,0:T(8,128)(2,1)}, u32[]{:S(2)}) copy-start(bf16[1,128,512]{2,1,0:T(8,128)(2,1)} %refs_3_.1) | copy-start | bytes 393220
  70.6 51.0 %copy-start.5 = (bf16[1,128,512]{2,1,0:T(8,128)(2,1)S(1)}, bf16[1,128,512]{2,1,0:T(8,128)(2,1)}, u32[]{:S(2)}) copy-start(bf16[1,128,512]{2,1,0:T(8,128)(2,1)} %refs_4_.1) | copy-start | bytes 393220

commit v6 on v5

--- a/solution.py
+++ b/solution.py
@@ -179,7 +179,7 @@
         product = jnp.concatenate([taps_re * real - taps_im * imag, taps_re * imag + taps_im * real], 1)
         timed = positions(product, 2 * CG, inv_mix, cos_turn, sin_turn, inv_full_ref)
         for row in range(2 * CG):
-            out_ref[pl.ds(seq * NB * 2 * CG + row, NB, 2 * CG), :] = timed[:, row * BLK : (row + 1) * BLK]
+            out_ref[row * CG * NB + seq * NB : row * CG * NB + (seq + 1) * NB, :] = timed[:, row * BLK : (row + 1) * BLK]
 
 
 def join_kernel(shares_ref, timed_ref, out_ref):
@@ -187,7 +187,7 @@
     lag = shares_ref[:peers, :] + shares_ref[peers : 2 * peers, :]
     lag = lag + (shares_ref[2 * peers : 3 * peers, :] + shares_ref[3 * peers :, :])
     for row in range(2 * CG):
-        out_ref[pl.ds(row, peers, OUT_ROWS), :] = timed_ref[pl.ds(row, peers, 2 * CG), :]
+        out_ref[pl.ds(row, peers, OUT_ROWS), :] = timed_ref[row * peers : (row + 1) * peers, :]
     for seq in range(CG):
         for part in range(CG):
             first = seq * NB * OUT_ROWS + 2 * CG + part

time: 123 us -> 123 us (level)
  no operation moved by 1% of the time
where the time goes in v6:
time: 123 us
  blocking collectives  106 us (86%)
  Pallas kernels  6.66 us (5%)
  waiting for transfers between devices  4.61 us (4%)
  starting transfers between devices  4.46 us (4%)
    all_to_all x2, blocking collectives, exchange(): lax.all_to_all(rows.reshape(peers, per, 1, BLK), ('zl', 'ctx'), 0, 0, til...  106 us
    all_to_all x1, waiting for transfers between devices, local(): lax.all_to_all(lag.reshape(4, peers, BLK), 'y', 0, 0, tiled=True)  4.61 us
    all_to_all x1, starting transfers between devices, local(): lax.all_to_all(lag.reshape(4, peers, BLK), 'y', 0, 0, tiled=True)  4.46 us
  transfers between devices with their start and end apart: 1, of which 1 were waited for; matrix products, arithmetic and copies ran while one was open for 0% of the time, Pallas kernels for 2%

profile of v6, /device:TPU:32, one launch (start us, length us, event | category | flops | bytes accessed | tf_op | source)
XLA Modules:
  0.0 122.6 jit_solution(11359175338230037186)
XLA Ops:
  0.6 0.0 copy-start
  0.6 0.0 copy-start.1
  0.7 0.0 copy-start.6
  0.7 0.0 copy-start.7
  0.7 0.0 copy-start.8
  0.7 0.0 copy-start.9
  0.7 1.4 %shard_map.146 = f32[1152,128]{1,0:T(8,128)S(1)} custom-call(bf16[1,128,512]{2,1,0:T(8,128)(2,1)} %refs_1_.1, bf16[1,128,512]{2,1,0:T(8,128)(2,1)} %refs_2_.1, bf16[1,128,512]{2,1,0:T(8,128)(2,1)} %refs_3_.1, bf16[1,128,512]{2,1,0:T(8,128)(2,1)} %refs_4_.1, f32[128,512]{1,0:T(8,128)} %taps_ref.1), custom_call_target="tpu_custom_call" | custom-call | tf_op jit(solution)/shard_map/pallas_call | solution.py:257
  2.2 55.1 %all_to_all.15 = f32[128,9,1,128]{3,2,1,0:T(1,128)S(1)} all-to-all(f32[128,9,1,128]{3,2,1,0:T(1,128)S(1)} %bitcast.10), channel_id=1, replica_groups=mesh['y'=4,'zl'=4,'ctx'=32] {'zl','ctx'}, dimensions={0} | all-to-all | bytes 1179648 | tf_op jit(solution)/shard_map/all_to_all | solution.py:244
  57.3 0.0 copy-done
  57.3 0.0 copy-done.1
  57.3 0.0 copy-done.6
  57.3 0.0 copy-done.7
  57.3 0.0 copy-done.8
  57.3 0.0 copy-done.9
  57.3 2.0 %shard_map.147 = (f32[1056,256]{1,0:T(8,128)S(1)}, f32[512,128]{1,0:T(8,128)}) custom-call(f32[1152,128]{1,0:T(8,128)S(1)} %bitcast.6, bf16[72,96]{1,0:T(8,128)(2,1)S(1)} %copy-done.8, f32[40,128]{1,0:T(8,128)S(1)} %copy-done.6, f32[40,128]{1,0:T(8,128)S(1)} %copy-done.7, bf16[768,256]{1,0:T(8,128)(2,1)S(1)} %copy-done, bf16[32,240]{1,0:T(8,128)(2,1)S(1)} %copy-done.9, ...), custom_call_target="tpu_custom_call" | custom-call | tf_op jit(solution)/shard_map/pallas_call | solution.py:261
  59.3 4.5 %all-to-all-start.1 = ((f32[4,128,128]{2,1,0:T(8,128)}), f32[4,128,128]{2,1,0:T(8,128)S(1)}, u32[]{:S(2)}, u32[]{:S(2)}) async-start(f32[4,128,128]{2,1,0:T(8,128)} %bitcast.2), calls=%async_computation.1 | async-start | bytes 524288 | tf_op jit(solution)/shard_map/all_to_all | solution.py:264
  63.8 2.1 %shard_map.148.timed_ref = f32[1024,128]{1,0:T(8,128)S(1)} custom-call(f32[1152,128]{1,0:T(8,128)S(1)} %bitcast.7, f32[1056,256]{1,0:T(8,128)S(1)} %get-tuple-element.8.both_ref, bf16[72,96]{1,0:T(8,128)(2,1)S(1)} %copy-done.8, f32[40,128]{1,0:T(8,128)S(1)} %copy-done.6, f32[40,128]{1,0:T(8,128)S(1)} %copy-done.7, bf16[768,256]{1,0:T(8,128)(2,1)S(1)} %copy-done, ...), custom_call_target="tpu_custom_call" | custom-call | tf_op jit(solution)/shard_map/pallas_call | solution.py:265
  65.9 4.6 %all-to-all-done.1 = f32[4,128,128]{2,1,0:T(8,128)S(1)} async-done(((f32[4,128,128]{2,1,0:T(8,128)}), f32[4,128,128]{2,1,0:T(8,128)S(1)}, u32[]{:S(2)}, u32[]{:S(2)}) %all-to-all-start.1) | async-done | bytes 262176 | tf_op jit(solution)/shard_map/all_to_all | solution.py:264
  70.5 0.1 shard_map.149
  70.6 0.0 copy-start.2
  70.6 0.0 copy-start.3
  70.6 0.0 copy-start.4
  70.6 0.0 copy-start.5
  70.6 50.9 %all_to_all.16 = f32[128,12,1,128]{3,2,1,0:T(1,128)S(1)} all-to-all(f32[128,12,1,128]{3,2,1,0:T(1,128)S(1)} %bitcast.9), channel_id=1, replica_groups=mesh['y'=4,'zl'=4,'ctx'=32] {'zl','ctx'}, dimensions={0} | all-to-all | bytes 1572864 | tf_op jit(solution)/shard_map/all_to_all | solution.py:244
  121.5 0.0 copy-done.2
  121.5 0.0 copy-done.3
  121.5 0.0 copy-done.4
  121.5 0.0 copy-done.5
  121.6 1.1 shard_map.150
Async XLA Ops:
  0.6 56.6 %copy-start = (bf16[768,256]{1,0:T(8,128)(2,1)S(1)}, bf16[768,256]{1,0:T(8,128)(2,1)}, u32[]{:S(2)}) copy-start(bf16[768,256]{1,0:T(8,128)(2,1)} %constant.16.clone.full_ref) | copy-start | bytes 1179652
  0.6 56.6 %copy-start.1 = (bf16[768,256]{1,0:T(8,128)(2,1)S(1)}, bf16[768,256]{1,0:T(8,128)(2,1)}, u32[]{:S(2)}) copy-start(bf16[768,256]{1,0:T(8,128)(2,1)} %constant.17.clone.inv_full_ref) | copy-start | bytes 1179652
  0.7 56.6 %copy-start.6 = (f32[40,128]{1,0:T(8,128)S(1)}, f32[40,128]{1,0:T(8,128)}, u32[]{:S(2)}) copy-start(f32[40,128]{1,0:T(8,128)} %constant.14.clone.cos_ref) | copy-start | bytes 61444
  0.7 56.6 %copy-start.7 = (f32[40,128]{1,0:T(8,128)S(1)}, f32[40,128]{1,0:T(8,128)}, u32[]{:S(2)}) copy-start(f32[40,128]{1,0:T(8,128)} %constant.15.clone.sin_ref) | copy-start | bytes 61444
  0.7 56.6 %copy-start.8 = (bf16[72,96]{1,0:T(8,128)(2,1)S(1)}, bf16[72,96]{1,0:T(8,128)(2,1)}, u32[]{:S(2)}) copy-start(bf16[72,96]{1,0:T(8,128)(2,1)} %constant.12.clone.mix_ref) | copy-start | bytes 41476
  0.7 56.6 %copy-start.9 = (bf16[32,240]{1,0:T(8,128)(2,1)S(1)}, bf16[32,240]{1,0:T(8,128)(2,1)}, u32[]{:S(2)}) copy-start(bf16[32,240]{1,0:T(8,128)(2,1)} %constant.13.clone.inv_mix_ref) | copy-start | bytes 46084
  59.3 11.1 %all-to-all-start.1 = ((f32[4,128,128]{2,1,0:T(8,128)}), f32[4,128,128]{2,1,0:T(8,128)S(1)}, u32[]{:S(2)}, u32[]{:S(2)}) async-start(f32[4,128,128]{2,1,0:T(8,128)} %bitcast.2), calls=%async_computation.1 | async-start | bytes 524288 | tf_op jit(solution)/shard_map/all_to_all | solution.py:264
  70.6 51.0 %copy-start.2 = (bf16[1,128,512]{2,1,0:T(8,128)(2,1)S(1)}, bf16[1,128,512]{2,1,0:T(8,128)(2,1)}, u32[]{:S(2)}) copy-start(bf16[1,128,512]{2,1,0:T(8,128)(2,1)} %refs_1_.1) | copy-start | bytes 393220
  70.6 51.0 %copy-start.3 = (bf16[1,128,512]{2,1,0:T(8,128)(2,1)S(1)}, bf16[1,128,512]{2,1,0:T(8,128)(2,1)}, u32[]{:S(2)}) copy-start(bf16[1,128,512]{2,1,0:T(8,128)(2,1)} %refs_2_.1) | copy-start | bytes 393220
  70.6 51.0 %copy-start.4 = (bf16[1,128,512]{2,1,0:T(8,128)(2,1)S(1)}, bf16[1,128,512]{2,1,0:T(8,128)(2,1)}, u32[]{:S(2)}) copy-start(bf16[1,128,512]{2,1,0:T(8,128)(2,1)} %refs_3_.1) | copy-start | bytes 393220
  70.6 51.0 %copy-start.5 = (bf16[1,128,512]{2,1,0:T(8,128)(2,1)S(1)}, bf16[1,128,512]{2,1,0:T(8,128)(2,1)}, u32[]{:S(2)}) copy-start(bf16[1,128,512]{2,1,0:T(8,128)(2,1)} %refs_4_.1) | copy-start | bytes 393220
